TPU v7x, 256 devices: a whole 4x4x8 slice. The times are simulated.
256 devices in a mesh: view: 16 (over z, y_hi), tok: 16 (over y_lo, x, core).
Axes of the slice: x: 4, y: 4 (y_hi: 2, y_lo: 2; y = y_hi * 2 + y_lo), z: 8, core: 2. Of those that a mesh axis runs over, the one named last changes fastest.
Arguments:
- q1: bfloat16 [16, 512, 1024], P('view', 'tok'), may hold values from -96 to 96
- k1: bfloat16 [16, 512, 1024], P('view', 'tok'), may hold values from -6 to 6
- v1: bfloat16 [16, 512, 1024], P('view', 'tok'), may hold values from -6 to 6
- nbr: int32 [16, 7], P('view'), may hold values from 0 to 15, as said below
- x2: bfloat16 [16, 512, 1024], P('view', 'tok'), may hold values from -6 to 6
- w_view_out: bfloat16 [1024, 1024], replicated, may hold values from -0.1875 to 0.1875
- norm_gain: float32 [1024], replicated, may hold values from 0.5 to 1.5
- w_qkv: bfloat16 [1024, 3072], replicated, may hold values from -0.1875 to 0.1875
- w_out: bfloat16 [1024, 1024], replicated, may hold values from -0.1875 to 0.1875
Outputs:
- view_feats: float32 [16, 512, 1024], P('view', 'tok')
- lrm_out: float32 [16, 512, 1024], P('view', 'tok')
Inputs may be any that keep to these rules, and one draw needn't show every extreme that they name: `nbr`: row v lists 7 distinct view indices, none equal to v.
All inputs are finite; a program needn't handle non-finite values.
Results may differ from a plain program's by a relative error of at most 0.014.
Values may be sent and summed in bfloat16 or wider, within the bound.
A program may use at most 128 MiB of HBM per device.

v0:
```python
import jax
import jax.numpy as jnp
from jax import lax
from jax.sharding import PartitionSpec as P

H1 = 16
HD1 = 64
HD2 = 64


EPSILON = 1e-06
NEGATIVE = -1e30


def absorb(running, queries, key_piece, val_piece, keep_key, factor_scale):
    running_max, row_total, weighted = running
    scores = (
        jnp.einsum("qhd,khd->qhk", queries, key_piece, preferred_element_type=jnp.float32)
        * factor_scale
    )
    scores = jnp.where(keep_key[None, None, :], scores, NEGATIVE)
    new_max = jnp.maximum(running_max, jnp.max(scores, axis=-1))
    weights = jnp.where(keep_key[None, None, :], jnp.exp(scores - new_max[..., None]), 0.0)
    row_total = jnp.sum(weights, axis=-1)
    weighted = jnp.einsum(
        "qhk,khd->qhd", weights.astype(jnp.bfloat16), val_piece, preferred_element_type=jnp.float32
    )
    return (new_max, row_total, weighted)


def per_device(q1, k1, v1, nbr, x2, w_view_out, norm_gain, w_qkv, w_out):
    own_view = lax.axis_index("view")
    wanted = nbr[0]
    queries = lax.all_gather(q1, "tok", axis=1, tiled=True)[0].reshape(-1, H1, HD1)
    query_rows = queries.shape[0]
    start_state = (
        jnp.full((query_rows, H1), NEGATIVE, jnp.float32),
        jnp.zeros((query_rows, H1), jnp.float32),
        jnp.zeros((query_rows, H1, HD1), jnp.float32),
    )
    scale_one = HD1 ** (-0.5)
    key_piece = lax.all_gather(k1, "view", axis=0, tiled=True)
    val_piece = lax.all_gather(v1, "view", axis=0, tiled=True)
    view_ids = jnp.arange(key_piece.shape[0], dtype=jnp.int32)
    keep_view = (view_ids == own_view) | jnp.any(view_ids[:, None] == wanted[None, :], axis=1)
    keep_key = jnp.repeat(keep_view, key_piece.shape[1])
    running_max, row_total, weighted = absorb(
        start_state,
        queries,
        key_piece.reshape(-1, H1, HD1),
        val_piece.reshape(-1, H1, HD1),
        keep_key,
        scale_one,
    )
    tok_devs = lax.axis_size("tok")
    my_rows = query_rows // tok_devs
    row_peak = lax.pmax(running_max, "tok")
    factor = jnp.exp(running_max - row_peak)
    summed, totals = (
        lax.psum_scatter(weighted * factor[..., None], "tok", scatter_dimension=0, tiled=True),
        lax.psum_scatter(row_total * factor, "tok", scatter_dimension=0, tiled=True),
    )
    attn_one = (summed / totals[..., None]).reshape(my_rows, -1)
    features = attn_one * lax.rsqrt(jnp.mean(attn_one * attn_one, axis=-1, keepdims=True) + EPSILON)
    features_half = features.astype(jnp.bfloat16)
    hidden = x2[0].astype(jnp.float32) + jnp.dot(
        features_half, w_view_out, preferred_element_type=jnp.float32
    )
    normed = (
        hidden * lax.rsqrt(jnp.mean(hidden * hidden, axis=-1, keepdims=True) + EPSILON) * norm_gain
    ).astype(jnp.bfloat16)
    projected = (
        jnp.dot(normed, w_qkv, preferred_element_type=jnp.float32)
        .astype(jnp.bfloat16)
        .reshape(my_rows, 3, -1)
    )
    by_head = lax.all_to_all(projected, "tok", split_axis=2, concat_axis=0, tiled=True)
    local_heads = by_head.shape[2] // HD2
    head_queries = by_head[:, 0].reshape(-1, local_heads, HD2)
    view_rows = head_queries.shape[0]
    scale_two = HD2 ** (-0.5)
    second_state = (
        jnp.full((view_rows, local_heads), NEGATIVE, jnp.float32),
        jnp.zeros((view_rows, local_heads), jnp.float32),
        jnp.zeros((view_rows, local_heads, HD2), jnp.float32),
    )
    key_piece = lax.all_gather(by_head[:, 1], "view", axis=0, tiled=True)
    val_piece = lax.all_gather(by_head[:, 2], "view", axis=0, tiled=True)
    keep_key = jnp.ones((key_piece.shape[0],), jnp.bool_)
    second_max, second_total, second_sum = absorb(
        second_state,
        head_queries,
        key_piece.reshape(-1, local_heads, HD2),
        val_piece.reshape(-1, local_heads, HD2),
        keep_key,
        scale_two,
    )
    attn_two = (second_sum / second_total[..., None]).reshape(view_rows, -1).astype(jnp.bfloat16)
    returned = lax.all_to_all(attn_two, "tok", split_axis=0, concat_axis=1, tiled=True)
    wide = returned.astype(jnp.float32)
    unit_rows = (wide * lax.rsqrt(jnp.mean(wide * wide, axis=-1, keepdims=True) + EPSILON)).astype(
        jnp.bfloat16
    )
    result = jnp.dot(unit_rows, w_out, preferred_element_type=jnp.float32)
    return (features[None], result[None])


def solution(mesh):
    return jax.shard_map(
        per_device,
        mesh=mesh,
        in_specs=(
            P("view", "tok", None),
            P("view", "tok", None),
            P("view", "tok", None),
            P("view", None),
            P("view", "tok", None),
            P(),
            P(),
            P(),
            P(),
        ),
        out_specs=(P("view", "tok", None), P("view", "tok", None)),
        check_vma=False,
    )
```

profile of v0, /device:TPU:1, one launch (start us, length us, event | category | flops | bytes accessed | tf_op | source)
XLA Modules:
  0.0 568.1 jit_solution(11776893962329701940)
XLA Ops:
  7.2 0.0 copy-start
  7.2 0.0 all-gather.8.cloned.1.call-start
  7.2 0.7 all-gather.8.cloned.1.call-update
  7.9 0.0 all-gather.10.cloned.1.call-start
  8.0 0.7 all-gather.10.cloned.1.call-update
  8.7 0.0 all-gather.12.cloned.1.call-start
  8.7 0.7 all-gather.12.cloned.1.call-update
  9.4 0.0 reduce-scatter.7.cloned.1.call-start
  9.4 0.7 fusion.49
  10.2 0.1 broadcast_in_dim.57
  10.3 0.1 broadcast_in_dim.58
  10.4 78.4 %all-gather.8.cloned.1.call-done = bf16[16,32,1024]{2,1,0:T(8,128)(2,1)} async-done(((bf16[1,32,1024]{2,1,0:T(8,128)(2,1)}), bf16[16,32,1024]{2,1,0:T(8,128)(2,1)}) %all-gather.8.cloned.1.call-update) | async-done | bytes 1048592 | tf_op jit(solution)/shard_map/all_gather | solution.py:42
  88.8 4.1 reshape.120
  92.8 33.8 %all-gather.10.cloned.1.call-done = bf16[1,512,1024]{2,1,0:T(8,128)(2,1)} async-done(((bf16[1,32,1024]{2,1,0:T(8,128)(2,1)}), bf16[1,512,1024]{2,1,0:T(8,128)(2,1)}) %all-gather.10.cloned.1.call-update) | async-done | bytes 1048592 | tf_op jit(solution)/shard_map/all_gather | solution.py:34
  126.6 1.5 copy.56
  128.1 9.1 %bitcast_reduce_fusion = (f32[512,16]{0,1:T(8,128)S(1)}, f32[16,512,512]{2,1,0:T(8,128)}) fusion(pred[512]{0:T(512)(128)(4,1)S(1)} %broadcast_in_dim.58, bf16[512,16,64]{0,2,1:T(8,128)(2,1)S(1)} %bitcast.104, bf16[512,16,64]{2,1,0:T(8,128)(2,1)} %reshape.120), kind=kOutput, calls=%fused_computation.3 | convolution fusion | flops 549445632 | bytes 18907648 | tf_op jit(solution)/shard_map/qhd,khd->qhk/dot_general | solution.py:18
  137.2 50.7 %pmax.7 = f32[512,16]{0,1:T(8,128)S(1)} all-reduce(f32[512,16]{0,1:T(8,128)S(1)} %broadcast_maximum_fusion), channel_id=1, replica_groups=mesh['view'=16,'tok'=16] {'tok'}, use_global_device_ids=true, to_apply=%region_2.3 | all-reduce | flops 8192 | bytes 65536 | tf_op jit(solution)/shard_map/pmax | solution.py:57
  187.8 8.2 %fusion.5 = f32[512,16]{0,1:T(8,128)S(1)} fusion(f32[16,512,512]{2,1,0:T(8,128)} %get-tuple-element.9, f32[512,16]{0,1:T(8,128)S(1)} %broadcast_maximum_fusion, pred[512]{0:T(512)(128)(4,1)S(1)} %broadcast_in_dim.58), kind=kLoop, calls=%fused_computation.10 | loop fusion | flops 20963328 | bytes 16843264 | tf_op jit(solution)/shard_map/reduce_sum | solution.py:24
  196.0 0.8 copy.73
  196.9 0.0 reduce-scatter.7.cloned.1.call-update
  196.9 0.0 reduce-scatter.5.cloned.1.call-start
  196.9 6.2 %all-gather.12.cloned.1.call-done = bf16[16,32,1024]{2,1,0:T(8,128)(2,1)} async-done(((bf16[1,32,1024]{2,1,0:T(8,128)(2,1)}), bf16[16,32,1024]{2,1,0:T(8,128)(2,1)}) %all-gather.12.cloned.1.call-update) | async-done | bytes 1048592 | tf_op jit(solution)/shard_map/all_gather | solution.py:43
  203.1 4.1 reshape.121
  207.1 0.0 copy-start.1
  207.1 0.0 copy-start.2
  207.1 11.6 %bitcast_multiply_fusion = f32[512,16,64]{0,2,1:T(8,128)} fusion(f32[16,512,512]{2,1,0:T(8,128)} %get-tuple-element.9, f32[512,16]{0,1:T(8,128)S(1)} %broadcast_maximum_fusion, pred[512]{0:T(512)(128)(4,1)S(1)} %broadcast_in_dim.58, bf16[512,16,64]{2,1,0:T(8,128)(2,1)} %reshape.121, f32[512,16]{0,1:T(8,128)S(1)} %get-tuple-element.5), kind=kOutput, calls=%fused_computation.21 | convolution fusion | flops 558366720 | bytes 19988992 | tf_op jit(solution)/shard_map/qhk,khd->qhd/dot_general | solution.py:25
  218.8 4.8 copy.60
  223.6 0.0 reduce-scatter.5.cloned.1.call-update
  223.6 0.2 all-gather.16.cloned.1.call-start
  223.9 42.9 %reduce-scatter.7.cloned.1.call-done = f32[32,16]{1,0:T(8,128)} async-done(((f32[512,16]{1,0:T(8,128)}), f32[32,16]{1,0:T(8,128)}) %reduce-scatter.7.cloned.1.call-update) | async-done | bytes 2064 | tf_op jit(solution)/shard_map/reduce_scatter | solution.py:61
  266.7 70.7 %reduce-scatter.5.cloned.1.call-done = f32[32,16,64]{2,1,0:T(8,128)} async-done(((f32[512,16,64]{2,1,0:T(8,128)}), f32[32,16,64]{2,1,0:T(8,128)}) %reduce-scatter.5.cloned.1.call-update) | async-done | bytes 131088 | tf_op jit(solution)/shard_map/reduce_scatter | solution.py:60
  337.4 1.5 multiply_reduce_fusion.1
  338.9 0.1 reshape.123
  339.1 0.0 copy-done
  339.1 0.0 copy-done.1
  339.1 0.6 multiply_reduce_fusion.2
  339.7 0.0 copy-done.2
  339.7 4.0 convolution_convert_fusion
  343.7 1.0 reshape.124
  344.7 1.8 copy.62
  346.5 1.4 reshape.133
  347.9 14.7 %all_to_all.28 = bf16[16,2,3072]{2,1,0:T(2,128)(2,1)} all-to-all(bf16[16,2,3072]{2,1,0:T(2,128)(2,1)} %reshape.133), channel_id=1, replica_groups=mesh['view'=16,'tok'=16] {'tok'}, dimensions={0} | all-to-all | bytes 393216 | tf_op jit(solution)/shard_map/all_to_all | solution.py:77
  362.6 1.6 reshape.134
  364.2 1.3 copy.72
  365.4 1.7 fusion.55
  367.1 0.0 all-gather.16.cloned.1.call-update
  367.1 0.0 all-gather.14.cloned.1.call-start
  367.2 0.7 all-gather.14.cloned.1.call-update
  367.9 0.1 reshape.122
  368.0 79.9 %all-gather.16.cloned.1.call-done = bf16[8192,1,64]{2,0,1:T(8,128)(2,1)} async-done(((bf16[512,1,64]{2,0,1:T(8,128)(2,1)}), bf16[8192,1,64]{2,0,1:T(8,128)(2,1)}) %all-gather.16.cloned.1.call-update) | async-done | bytes 1048592 | tf_op jit(solution)/shard_map/all_gather | solution.py:87
  447.9 9.6 %multiply_reduce_fusion = (f32[512]{0:T(512)S(1)}, f32[8192,512]{1,0:T(8,128)}) fusion(bf16[512,3,64]{2,0,1:T(8,128)(2,1)} %bitcast.108, bf16[8192,1,64]{2,0,1:T(8,128)(2,1)} %all-gather.16.cloned.1.call-done), kind=kOutput, calls=%fused_computation.7 | convolution fusion | flops 545259008 | bytes 19007488 | tf_op jit(solution)/shard_map/qhd,khd->qhk/dot_general | solution.py:18
  457.6 8.6 %fusion.3 = f32[512]{0:T(512)S(1)} fusion(f32[8192,512]{1,0:T(8,128)} %get-tuple-element.13, f32[512]{0:T(512)S(1)} %broadcast_maximum_fusion.1), kind=kLoop, calls=%fused_computation.8 | loop fusion | flops 12582400 | bytes 16781312 | tf_op jit(solution)/shard_map/reduce_sum | solution.py:24
  466.2 67.0 %all-gather.14.cloned.1.call-done = bf16[8192,1,64]{2,0,1:T(8,128)(2,1)} async-done(((bf16[512,1,64]{2,0,1:T(8,128)(2,1)}), bf16[8192,1,64]{2,0,1:T(8,128)(2,1)}) %all-gather.14.cloned.1.call-update) | async-done | bytes 1048592 | tf_op jit(solution)/shard_map/all_gather | solution.py:88
  533.2 9.3 %fusion.39 = bf16[512,1,64]{0,2,1:T(8,128)(2,1)S(1)} fusion(f32[8192,512]{1,0:T(8,128)} %get-tuple-element.13, f32[512]{0:T(512)S(1)} %broadcast_maximum_fusion.1, bf16[8192,1,64]{2,0,1:T(8,128)(2,1)} %all-gather.14.cloned.1.call-done, f32[512]{0:T(512)S(1)} %fusion.3), kind=kOutput, calls=%fused_computation.30 | convolution fusion | flops 549519360 | bytes 17895424 | tf_op jit(solution)/shard_map/qhk,khd->qhd/dot_general | solution.py:25
  542.5 0.1 copy.68
  542.7 0.8 reshape.135
  543.4 8.6 %all-to-all-start.1 = ((bf16[16,2,1024]{2,1,0:T(2,128)(2,1)}), bf16[16,2,1024]{2,1,0:T(2,128)(2,1)S(1)}, u32[]{:S(2)}, u32[]{:S(2)}) async-start(bf16[16,2,1024]{2,1,0:T(2,128)(2,1)} %reshape.135), calls=%async_computation.2 | async-start | bytes 131072 | tf_op jit(solution)/shard_map/all_to_all | solution.py:99
  552.0 0.7 broadcast_multiply_fusion
  552.8 5.1 all-to-all-done.1
  557.8 0.1 reshape.136
  558.0 0.1 fusion.44
  558.2 0.2 copy.69
  558.3 0.1 reshape.128
  558.5 2.8 convolution_bitcast_fusion
  (8 shorter events, 0.1 us)
Async XLA Ops:
  7.2 331.9 %copy-start = (bf16[1024,1024]{1,0:T(8,128)(2,1)S(1)}, bf16[1024,1024]{1,0:T(8,128)(2,1)}, u32[]{:S(2)}) copy-start(bf16[1024,1024]{1,0:T(8,128)(2,1)} %param.14) | copy-start | bytes 6291460
  7.2 81.6 %all-gather.8.cloned.1.call-start = ((), (), s32[]{:S(2)}) async-start(), calls=%async_computation.4 | async-start | bytes 1114112 | tf_op jit(solution)/shard_map/all_gather | solution.py:42
  7.9 118.7 %all-gather.10.cloned.1.call-start = ((), (), s32[]{:S(2)}) async-start(), calls=%async_computation.5 | async-start | bytes 1114112 | tf_op jit(solution)/shard_map/all_gather | solution.py:34
  8.7 194.4 %all-gather.12.cloned.1.call-start = ((), (), s32[]{:S(2)}) async-start(), calls=%async_computation.6 | async-start | bytes 1114112 | tf_op jit(solution)/shard_map/all_gather | solution.py:43
  9.4 257.3 %reduce-scatter.7.cloned.1.call-start = ((), (), s32[]{:S(2)}) async-start(), calls=%async_computation.10 | async-start | bytes 278528 | tf_op jit(solution)/shard_map/reduce_scatter | solution.py:61
  196.9 140.5 %reduce-scatter.5.cloned.1.call-start = ((), (), s32[]{:S(2)}) async-start(), calls=%async_computation.7 | async-start | bytes 4456448 | tf_op jit(solution)/shard_map/reduce_scatter | solution.py:60
  207.1 131.9 %copy-start.1 = (bf16[1,32,1024]{2,1,0:T(8,128)(2,1)S(1)}, bf16[1,32,1024]{2,1,0:T(8,128)(2,1)}, u32[]{:S(2)}) copy-start(bf16[1,32,1024]{2,1,0:T(8,128)(2,1)} %param.13) | copy-start | bytes 196612
  207.1 132.6 %copy-start.2 = (f32[1024]{0:T(1024)S(1)}, f32[1024]{0:T(1024)}, u32[]{:S(2)}) copy-start(f32[1024]{0:T(1024)} %param.15) | copy-start | bytes 12292
  223.6 224.3 %all-gather.16.cloned.1.call-start = ((), (), s32[]{:S(2)}) async-start(), calls=%async_computation.9 | async-start | bytes 2228224 | tf_op jit(solution)/shard_map/all_gather | solution.py:87
  367.1 166.1 %all-gather.14.cloned.1.call-start = ((), (), s32[]{:S(2)}) async-start(), calls=%async_computation.8 | async-start | bytes 2228224 | tf_op jit(solution)/shard_map/all_gather | solution.py:88
  543.4 14.4 %all-to-all-start.1 = ((bf16[16,2,1024]{2,1,0:T(2,128)(2,1)}), bf16[16,2,1024]{2,1,0:T(2,128)(2,1)S(1)}, u32[]{:S(2)}, u32[]{:S(2)}) async-start(bf16[16,2,1024]{2,1,0:T(2,128)(2,1)} %reshape.135), calls=%async_computation.2 | async-start | bytes 131072 | tf_op jit(solution)/shard_map/all_to_all | solution.py:99
Sparse Core Ops, SparseCore 0:
  10.6 78.1 all-gather.7
  90.6 35.9 all-gather.9
  129.2 73.8 all-gather.11
  205.4 61.2 reduce-scatter.6
  269.1 68.2 reduce-scatter.4
  367.3 80.6 all-gather.15
  451.1 82.0 all-gather.13
where the time goes:
time: 569 us; the launch traced here: 568 us
  waiting for transfers between devices  387 us (68%)
  blocking collectives  65.4 us (11%)
  matrix products  47.1 us (8%)
  local copies, waits for them, and re-layouts  25.7 us (5%)
  other arithmetic  20 us (4%)
  between operations  14.3 us (3%)
  starting transfers between devices  9.04 us (2%)
    all_gather x1, waiting for transfers between devices, per_device(): key_piece = lax.all_gather(by_head[:, 1], 'view', axis=0, tiled=True)  79.9 us
    all_gather x1, waiting for transfers between devices, per_device(): key_piece = lax.all_gather(k1, 'view', axis=0, tiled=True)  78.4 us
    reduce_scatter x1, waiting for transfers between devices, per_device(): lax.psum_scatter(weighted * factor[..., None], 'tok', scatter_dimension=0...  70.7 us
    all_gather x1, waiting for transfers between devices, per_device(): val_piece = lax.all_gather(by_head[:, 2], 'view', axis=0, tiled=True)  67 us
    pmax x1, blocking collectives, per_device(): row_peak = lax.pmax(running_max, 'tok')  50.7 us
    reduce_scatter x1, waiting for transfers between devices, per_device(): lax.psum_scatter(row_total * factor, 'tok', scatter_dimension=0, tiled=True)  42.9 us
    all_gather x1, waiting for transfers between devices, per_device(): lax.all_gather(q1, 'tok', axis=1, tiled=True)[0].reshape(-1, H1, HD1)  33.8 us
    dot_general x2, matrix products, absorb(): jnp.einsum('qhk,khd->qhd', weights.astype(jnp.bfloat16), val_piece, prefe...  21 us
  transfers between devices with their start and end apart: 8, of which 8 were waited for; matrix products, arithmetic and copies ran while one was open for 11% of the time, Pallas kernels for 0%

commit v1 on v0

v1 whole, which is shorter than its diff:
```python
import math

import jax
import jax.numpy as jnp
from jax import lax
from jax.experimental import pallas as pl
from jax.experimental.pallas import tpu as pltpu
from jax.sharding import PartitionSpec as P

MESH = pl.DeviceIdType.MESH
BF = jnp.bfloat16
F32 = jnp.float32

EPSILON = 1e-06
NEGATIVE = -1e30
START_MAX = -3e38
HD = 64
LANES = 2 * HD
Z = 8
HEADS = 16
TOKS = 16
MY_ROWS = 32
WIDTH = HEADS * HD
ROWS = TOKS * MY_ROWS
VIEWS = 2 * Z
SUB = 4
PIECE = ROWS // SUB
EXP2_SCALE = HD ** (-0.5) * math.log2(math.e)


def wait_bytes(like, sem):
    pltpu.make_async_copy(like, like, sem).wait()


def rows_of(ref, start, count):
    return ref.at[pl.ds(pl.multiple_of(start, count if count < 128 else 128), count), :]


def pack(q_of, k_of, v_of, extra, sq, skv):
    low = lax.broadcasted_iota(jnp.int32, (MY_ROWS, LANES), 1) < HD
    for pair in range(HEADS // 2):
        q, k, v = q_of(pair), k_of(pair), v_of(pair)
        turned_q, turned_k, turned_v = (pltpu.roll(part, HD, 1) for part in (q, k, v))
        first, second = 2 * pair * MY_ROWS, (2 * pair + 1) * MY_ROWS
        sq[first : first + MY_ROWS, :] = jnp.where(low, q, extra).astype(BF)
        sq[second : second + MY_ROWS, :] = jnp.where(low, turned_q, extra).astype(BF)
        skv[first : first + MY_ROWS, :] = jnp.where(low, k, turned_v).astype(BF)
        skv[second : second + MY_ROWS, :] = jnp.where(low, turned_k, v).astype(BF)


def kernel(
    nbr, q1, k1, v1, x2, w_view_out, norm_gain, w_qkv, w_out,
    feats_out, lrm_out,
    q_in, k_in, v_in, x_in, gain_in, wv, wqkv, wo,
    sq_one, skv_one, qb_one, kv_one, so_one, ro_one,
    sq_two, skv_two, qb_two, kv_two, so_two, ro_two,
    peak, acc, feats, result,
    load_sem, weight_sem, out_sem, a2a_send, a2a_q, a2a_kv, ring_send, ring_recv, pair_send, pair_recv, back_send, back_recv,
):
    view = lax.axis_index("view")
    tok = lax.axis_index("tok")
    z, y_hi = view // 2, view % 2
    core = tok % 2
    my_head = y_hi * 8 + tok // 8 * 4 + tok // 2 % 4
    my_view = z * 2 + core
    at_home = core == y_hi
    right = (z + 1) % Z * 2 + y_hi
    left = (z + Z - 1) % Z * 2 + y_hi
    partner = tok + 1 - 2 * core

    loads = [
        pltpu.make_async_copy(src, dst, load_sem.at[i])
        for i, (src, dst) in enumerate(
            ((q1.at[0], q_in), (k1.at[0], k_in), (v1.at[0], v_in), (x2.at[0], x_in), (norm_gain, gain_in))
        )
    ]
    weights = [
        pltpu.make_async_copy(src, dst, weight_sem.at[i])
        for i, (src, dst) in enumerate(((w_view_out, wv), (w_qkv, wqkv), (w_out, wo)))
    ]
    for copy in loads:
        copy.start()

    def head_device(head):
        return (z * 2 + head // 8, head // 4 % 2 * 8 + head % 4 * 2 + y_hi)

    def row_device(member):
        return (my_view, member)

    barrier = pltpu.get_barrier_semaphore()

    def greet(i, _):
        head_view, head_tok = head_device(i)

        @pl.when(jnp.logical_or(head_view != view, head_tok != tok))
        def _():
            pl.semaphore_signal(barrier, inc=1, device_id=(head_view, head_tok), device_id_type=MESH)

        @pl.when(jnp.logical_or(my_view != view, i != tok))
        def _():
            pl.semaphore_signal(barrier, inc=1, device_id=(my_view, i), device_id_type=MESH)

        return 0

    lax.fori_loop(0, TOKS, greet, 0)
    pl.semaphore_signal(barrier, inc=1, device_id=(right, tok), device_id_type=MESH)
    pl.semaphore_signal(barrier, inc=1, device_id=(left, tok), device_id_type=MESH)
    pl.semaphore_signal(barrier, inc=1, device_id=(view, partner), device_id_type=MESH)

    for copy in weights:
        copy.start()

    lane = lax.broadcasted_iota(jnp.int32, (1, LANES), 1)
    low_ones = jnp.where(lane < HD, 1.0, 0.0).astype(BF)
    high_ones = jnp.where(lane < HD, 0.0, 1.0).astype(BF)

    def all_to_all(stage, sq, skv, qb, kv):
        def send(i, _):
            head = (my_head + i) % HEADS
            head_view, head_tok = head_device(head)
            mine = jnp.logical_and(head_view == view, head_tok == tok)
            src_q = rows_of(sq, head * MY_ROWS, MY_ROWS)
            dst_q = rows_of(qb, tok * MY_ROWS, MY_ROWS)
            src_kv = rows_of(skv, head * MY_ROWS, MY_ROWS)
            dst_kv = rows_of(kv, view * ROWS + tok * MY_ROWS, MY_ROWS)
            sem_kv = a2a_kv.at[stage, tok * MY_ROWS // PIECE]

            @pl.when(mine)
            def _():
                pltpu.make_async_copy(src_kv, dst_kv, sem_kv).start()
                pltpu.make_async_copy(src_q, dst_q, a2a_q.at[stage]).start()

            @pl.when(jnp.logical_not(mine))
            def _():
                for src, dst, sem, k in ((src_kv, dst_kv, sem_kv, 0), (src_q, dst_q, a2a_q.at[stage], 1)):
                    pltpu.make_async_remote_copy(
                        src_ref=src,
                        dst_ref=dst,
                        send_sem=a2a_send.at[stage, k],
                        recv_sem=sem,
                        device_id=(head_view, head_tok),
                        device_id_type=MESH,
                    ).start()

            return 0

        lax.fori_loop(0, HEADS, send, 0)

    def sent(like, sem):
        @pl.when(at_home)
        def _():
            wait_bytes(like.at[pl.ds(0, (HEADS - 1) * MY_ROWS), :], sem)

        @pl.when(jnp.logical_not(at_home))
        def _():
            wait_bytes(like.at[pl.ds(0, HEADS * MY_ROWS), :], sem)

    def ring_piece(stage, kv, direction, step, sub):
        from_z = (z + Z - step) % Z if direction == 0 else (z + step) % Z
        block = rows_of(kv, (from_z * 2 + core) * ROWS + sub * PIECE, PIECE)
        pltpu.make_async_remote_copy(
            src_ref=block,
            dst_ref=block,
            send_sem=ring_send.at[stage, direction],
            recv_sem=ring_recv.at[stage, direction, step * SUB + sub],
            device_id=(right if direction == 0 else left, tok),
            device_id_type=MESH,
        ).start()

    def to_partner(stage, kv, from_z, sub, slot):
        block = rows_of(kv, (from_z * 2 + core) * ROWS + sub * PIECE, PIECE)
        pltpu.make_async_remote_copy(
            src_ref=block,
            dst_ref=block,
            send_sem=pair_send.at[stage],
            recv_sem=pair_recv.at[stage, slot],
            device_id=(view, partner),
            device_id_type=MESH,
        ).start()

    def absorb(kv, qb, which, masked):
        block = kv[pl.ds(pl.multiple_of(which * ROWS, ROWS), ROWS), :]
        keys = block
        if masked:
            hot = jnp.where(lane == HD + which, 1.0, 0.0).astype(BF)
            keys = block * low_ones + hot
        values = block * high_ones + low_ones
        for half in range(2):
            cols = slice(half * (ROWS // 2), (half + 1) * (ROWS // 2))
            scores = lax.dot_general(
                keys, qb[cols, :], (((1,), (1,)), ((), ())), preferred_element_type=F32
            )
            old = peak[:, cols]
            new = jnp.maximum(old, jnp.max(scores, axis=0, keepdims=True))
            factor = jnp.exp2((old - new) * EXP2_SCALE)
            weights16 = jnp.exp2((scores - new) * EXP2_SCALE).astype(BF)
            part = lax.dot_general(
                values, weights16, (((0,), (0,)), ((), ())), preferred_element_type=F32
            )
            acc[:, cols] = acc[:, cols] * factor + part
            peak[:, cols] = new

    def attend(stage, qb, kv, masked):
        peak[...] = jnp.full_like(peak, START_MAX)
        acc[...] = jnp.zeros_like(acc)
        for sub in range(SUB):
            wait_bytes(rows_of(kv, my_view * ROWS + sub * PIECE, PIECE), a2a_kv.at[stage, sub])
            ring_piece(stage, kv, 0, 0, sub)
            ring_piece(stage, kv, 1, 0, sub)
            to_partner(stage, kv, z, sub, 0)
        wait_bytes(qb, a2a_q.at[stage])

        def piece_of(step, sub, direction):
            from_z = (z + Z - step) % Z if direction == 0 else (z + step) % Z
            slot = 2 * step - 1 + direction
            block = rows_of(kv, (from_z * 2 + core) * ROWS + sub * PIECE, PIECE)
            wait_bytes(block, ring_recv.at[stage, direction, (step - 1) * SUB + sub])
            if direction == 0:
                go_on = jnp.logical_or(step < Z // 2 - 1, sub < SUB // 2)
            else:
                go_on = jnp.logical_or(step < Z // 2 - 1, sub >= SUB // 2)

            @pl.when(jnp.logical_and(step < Z // 2, go_on))
            def _():
                ring_piece(stage, kv, direction, step, sub)

            to_partner(stage, kv, from_z, sub, jnp.minimum(slot, Z - 1))

        def step_of(i, _):
            step, sub = i // SUB + 1, i % SUB
            last = step == Z // 2

            @pl.when(jnp.logical_or(jnp.logical_not(last), sub < SUB // 2))
            def _():
                piece_of(step, sub, 0)

            @pl.when(jnp.logical_or(jnp.logical_not(last), sub >= SUB // 2))
            def _():
                piece_of(step, sub, 1)

            @pl.when(jnp.logical_or(step > 1, sub < 2))
            def _():
                direction, other = sub % 2, sub // 2
                first = step == 1
                behind = step - 1
                from_z = jnp.where(direction == 0, (z + Z - behind) % Z, (z + behind) % Z)
                use_other = jnp.where(first, sub, other)
                whose = core + use_other * (1 - 2 * core)
                which = jnp.where(first, z, from_z) * 2 + whose
                slot = jnp.where(first, 0, 2 * behind - 1 + direction)

                @pl.when(use_other == 1)
                def _():
                    wait_bytes(rows_of(kv, which * ROWS, ROWS), pair_recv.at[stage, slot])

                absorb(kv, qb, which, masked)

            return 0

        lax.fori_loop(0, Z // 2 * SUB, step_of, 0)
        far = (z + Z // 2) % Z * 2

        def last_two(i, _):
            which = far + core + i * (1 - 2 * core)

            @pl.when(i == 1)
            def _():
                wait_bytes(rows_of(kv, which * ROWS, ROWS), pair_recv.at[stage, Z - 1])

            absorb(kv, qb, which, masked)
            return 0

        lax.fori_loop(0, 2, last_two, 0)

    def ring_sent(stage, kv):
        for direction in range(2):
            wait_bytes(kv.at[pl.ds(0, ((Z // 2 - 1) * SUB + SUB // 2) * PIECE), :], ring_send.at[stage, direction])
        wait_bytes(kv.at[pl.ds(0, Z * ROWS), :], pair_send.at[stage])

    def send_back(stage, so, ro):
        whole = acc[...]
        so[...] = jnp.transpose(whole * (1.0 / whole[0:1, :])).astype(BF)

        def send(i, _):
            member = (tok + i) % TOKS
            mine = jnp.logical_and(my_view == view, member == tok)
            src = rows_of(so, member * MY_ROWS, MY_ROWS)
            dst = rows_of(ro, my_head * MY_ROWS, MY_ROWS)

            @pl.when(mine)
            def _():
                pltpu.make_async_copy(src, dst, back_recv.at[stage]).start()

            @pl.when(jnp.logical_not(mine))
            def _():
                pltpu.make_async_remote_copy(
                    src_ref=src,
                    dst_ref=dst,
                    send_sem=back_send.at[stage],
                    recv_sem=back_recv.at[stage],
                    device_id=(my_view, member),
                    device_id_type=MESH,
                ).start()

            return 0

        lax.fori_loop(0, TOKS, send, 0)
        wait_bytes(ro, back_recv.at[stage])

    def side_by_side(ro):
        low = lax.broadcasted_iota(jnp.int32, (MY_ROWS, LANES), 1) < HD
        parts = []
        for pair in range(HEADS // 2):
            first = ro[2 * pair * MY_ROWS : (2 * pair + 1) * MY_ROWS, :].astype(F32)
            second = ro[(2 * pair + 1) * MY_ROWS : (2 * pair + 2) * MY_ROWS, :].astype(F32)
            parts.append(jnp.where(low, pltpu.roll(first, HD, 1), second))
        return jnp.concatenate(parts, axis=1)

    def unit(values):
        return values * lax.rsqrt(jnp.mean(values * values, axis=-1, keepdims=True) + EPSILON)

    for copy in loads[:3]:
        copy.wait()
    lanes = lax.broadcasted_iota(jnp.int32, (MY_ROWS, LANES), 1)
    wanted = lanes == HD + view
    for i in range(nbr.shape[1]):
        wanted = jnp.logical_or(wanted, lanes == HD + nbr[0, i])
    bias = jnp.where(jnp.logical_or(wanted, lanes >= HD + VIEWS), 0.0, NEGATIVE)

    def cut(ref):
        return lambda pair: ref[:, pair * LANES : (pair + 1) * LANES].astype(F32)

    pack(cut(q_in), cut(k_in), cut(v_in), bias, sq_one, skv_one)
    pl.semaphore_wait(barrier, jnp.where(at_home, 2 * TOKS + 1, 2 * TOKS + 3))
    all_to_all(0, sq_one, skv_one, qb_one, kv_one)
    attend(0, qb_one, kv_one, True)
    send_back(0, so_one, ro_one)

    attn = side_by_side(ro_one)
    feats_f32 = unit(attn)
    feats[...] = feats_f32
    feats_copy = pltpu.make_async_copy(feats, feats_out.at[0], out_sem.at[0])
    feats_copy.start()
    for copy in loads[3:]:
        copy.wait()
    weights[0].wait()
    hidden = x_in[...].astype(F32) + jnp.dot(feats_f32.astype(BF), wv[...], preferred_element_type=F32)
    normed = (unit(hidden) * gain_in[...]).astype(BF)
    weights[1].wait()
    projected = [
        jnp.dot(normed, wqkv[:, part * WIDTH : (part + 1) * WIDTH], preferred_element_type=F32)
        for part in range(3)
    ]

    def cut_value(value):
        return lambda pair: value[:, pair * LANES : (pair + 1) * LANES]

    pack(*(cut_value(part) for part in projected), jnp.zeros((MY_ROWS, LANES), F32), sq_two, skv_two)

    all_to_all(1, sq_two, skv_two, qb_two, kv_two)
    attend(1, qb_two, kv_two, False)
    send_back(1, so_two, ro_two)
    unit_rows = unit(side_by_side(ro_two)).astype(BF)
    weights[2].wait()
    result[...] = jnp.dot(unit_rows, wo[...], preferred_element_type=F32)
    result_copy = pltpu.make_async_copy(result, lrm_out.at[0], out_sem.at[1])
    result_copy.start()

    for stage, (sq, skv, kv, so) in enumerate(
        ((sq_one, skv_one, kv_one, so_one), (sq_two, skv_two, kv_two, so_two))
    ):
        sent(skv, a2a_send.at[stage, 0])
        sent(sq, a2a_send.at[stage, 1])
        ring_sent(stage, kv)
        sent(so, back_send.at[stage])
    feats_copy.wait()
    result_copy.wait()


def per_device(q1, k1, v1, nbr, x2, w_view_out, norm_gain, w_qkv, w_out):
    anywhere = pl.BlockSpec(memory_space=pl.ANY)
    dma = pltpu.SemaphoreType.DMA
    stage_buffers = [
        pltpu.VMEM((ROWS, LANES), BF),
        pltpu.VMEM((ROWS, LANES), BF),
        pltpu.VMEM((ROWS, LANES), BF),
        pltpu.VMEM((VIEWS * ROWS, LANES), BF),
        pltpu.VMEM((ROWS, LANES), BF),
        pltpu.VMEM((ROWS, LANES), BF),
    ]
    return tuple(pl.pallas_call(
        kernel,
        out_shape=(
            jax.ShapeDtypeStruct((1, MY_ROWS, WIDTH), F32),
            jax.ShapeDtypeStruct((1, MY_ROWS, WIDTH), F32),
        ),
        in_specs=[pl.BlockSpec(memory_space=pltpu.SMEM)] + [anywhere] * 8,
        out_specs=(anywhere, anywhere),
        scratch_shapes=[pltpu.VMEM((MY_ROWS, WIDTH), BF)] * 4
        + [
            pltpu.VMEM((1, WIDTH), F32),
            pltpu.VMEM((WIDTH, WIDTH), BF),
            pltpu.VMEM((WIDTH, 3 * WIDTH), BF),
            pltpu.VMEM((WIDTH, WIDTH), BF),
        ]
        + stage_buffers * 2
        + [
            pltpu.VMEM((1, ROWS), F32),
            pltpu.VMEM((LANES, ROWS), F32),
            pltpu.VMEM((MY_ROWS, WIDTH), F32),
            pltpu.VMEM((MY_ROWS, WIDTH), F32),
            dma((5,)),
            dma((3,)),
            dma((2,)),
            dma((2, 2)),
            dma((2,)),
            dma((2, SUB)),
            dma((2, 2)),
            dma((2, 2, Z // 2 * SUB)),
            dma((2,)),
            dma((2, Z)),
            dma((2,)),
            dma((2,)),
        ],
        compiler_params=pltpu.CompilerParams(
            collective_id=0, has_side_effects=True, vmem_limit_bytes=56 * 1024 * 1024
        ),
    )(nbr, q1, k1, v1, x2, w_view_out, norm_gain.reshape(1, -1), w_qkv, w_out))


def solution(mesh):
    return jax.shard_map(
        per_device,
        mesh=mesh,
        in_specs=(
            P("view", "tok", None),
            P("view", "tok", None),
            P("view", "tok", None),
            P("view", None),
            P("view", "tok", None),
            P(),
            P(),
            P(),
            P(),
        ),
        out_specs=(P("view", "tok", None), P("view", "tok", None)),
        check_vma=False,
    )
```

time: 569 us -> 85.7 us (0.15)
  waiting for transfers between devices: 387 us -> 0 us
  Pallas kernels: 0 us -> 81.8 us
  blocking collectives: 65.4 us -> 0 us
  matrix products: 47.1 us -> 0 us
  local copies, waits for them, and re-layouts: 25.7 us -> 3.14 us
  other arithmetic: 20 us -> 0 us
  between operations: 14.3 us -> 0.64 us
  starting transfers between devices: 9.04 us -> 0 us
    all_gather x5 -> x0, waiting for transfers between devices: 265 us -> none  [the longest x1 79.9 us: per_device(): key_piece = lax.all_gather(by_head[:, 1], 'view', axis=0, tiled=True)]
    reduce_scatter x2 -> x0, waiting for transfers between devices: 114 us -> none  [the longest x1 70.7 us: per_device(): lax.psum_scatter(weighted * factor[..., None], 'tok', scatter_dimension=0...]
    pallas_call x0 -> x1, Pallas kernels: none -> 81.8 us  [per_device(): pl.pallas_call(kernel, out_shape=(jax.ShapeDtypeStruct((1, MY_ROWS, WIDTH...]
    pmax x1 -> x0, blocking collectives: 50.7 us -> none  [per_device(): row_peak = lax.pmax(running_max, 'tok')]
    dot_general x7 -> x0, matrix products: 47.1 us -> none  [the longest x2 21 us: absorb(): jnp.einsum('qhk,khd->qhd', weights.astype(jnp.bfloat16), val_piece, prefe...]
    reduce_sum x4 -> x0, other arithmetic: 18.4 us -> none  [the longest x2 16.7 us: absorb(): row_total = jnp.sum(weights, axis=-1)]
    all_to_all x1 -> x0, blocking collectives: 14.7 us -> none  [per_device(): lax.all_to_all(projected, 'tok', split_axis=2, concat_axis=0, tiled=True)]
    reshape x6 -> x0, local copies, waits for them, and re-layouts: 11.1 us -> none  [the longest x1 4.05 us: per_device(): key_piece.reshape(-1, H1, HD1)]
  transfers between devices with their start and end apart: 8 -> 0, of which waited for: 8 -> 0; matrix products, arithmetic and copies ran while one was open for 11% -> 0% of each run, Pallas kernels for 0% -> 0%
where the time goes in v1:
time: 85.7 us; the launch traced here: 85.6 us
  Pallas kernels  81.8 us (95%)
  local copies, waits for them, and re-layouts  3.14 us (4%)
    pallas_call x1, Pallas kernels, per_device(): pl.pallas_call(kernel, out_shape=(jax.ShapeDtypeStruct((1, MY_ROWS, WIDTH...  81.8 us
    unnamed x2, local copies, waits for them, and re-layouts  3.14 us

profile of v1, /device:TPU:1, one launch (start us, length us, event | category | flops | bytes accessed | tf_op | source)
XLA Modules:
  0.0 85.6 jit_solution(11802952877070500629)
XLA Ops:
  0.6 81.8 %shard_map.104 = (f32[1,32,1024]{2,1,0:T(8,128)}, f32[1,32,1024]{2,1,0:T(8,128)}) custom-call(s32[1,7]{1,0:T(1,128)} %nbr.1, bf16[1,32,1024]{2,1,0:T(8,128)(2,1)} %q1.1, bf16[1,32,1024]{2,1,0:T(8,128)(2,1)} %k1.1, bf16[1,32,1024]{2,1,0:T(8,128)(2,1)} %v1.1, bf16[1,32,1024]{2,1,0:T(8,128)(2,1)} %x2.1, bf16[1024,1024]{1,0:T(8,128)(2,1)} %w_view_out.1, ...), custom_call_target="tpu_custom_call" | custom-call | tf_op jit(solution)/shard_map/pallas_call | solution.py:391
  82.4 1.6 %copy.13 = f32[1,32,1024]{2,1,0:T(8,128)} copy(f32[1,32,1024]{2,1,0:T(8,128)} %get-tuple-element.4) | data formatting | bytes 262144
  84.0 1.6 %copy.14 = f32[1,32,1024]{2,1,0:T(8,128)} copy(f32[1,32,1024]{2,1,0:T(8,128)} %get-tuple-element.5) | data formatting | bytes 262144

commit v2 on v1

--- a/solution.py
+++ b/solution.py
@@ -20,6 +20,7 @@
 HEADS = 16
 TOKS = 16
 MY_ROWS = 32
+HALF = MY_ROWS // 2
 WIDTH = HEADS * HD
 ROWS = TOKS * MY_ROWS
 VIEWS = 2 * Z
@@ -36,14 +37,15 @@
     return ref.at[pl.ds(pl.multiple_of(start, count if count < 128 else 128), count), :]
 
 
-def pack(q_of, k_of, v_of, extra, sq, skv):
+def pack(q_of, k_of, v_of, sq, skv):
     low = lax.broadcasted_iota(jnp.int32, (MY_ROWS, LANES), 1) < HD
+    low_half = lax.broadcasted_iota(jnp.int32, (HALF, LANES), 1) < HD
     for pair in range(HEADS // 2):
         q, k, v = q_of(pair), k_of(pair), v_of(pair)
         turned_q, turned_k, turned_v = (pltpu.roll(part, HD, 1) for part in (q, k, v))
         first, second = 2 * pair * MY_ROWS, (2 * pair + 1) * MY_ROWS
-        sq[first : first + MY_ROWS, :] = jnp.where(low, q, extra).astype(BF)
-        sq[second : second + MY_ROWS, :] = jnp.where(low, turned_q, extra).astype(BF)
+        sq[2 * pair * HALF : (2 * pair + 1) * HALF, :] = jnp.where(low_half, q[:HALF], turned_q[HALF:]).astype(BF)
+        sq[(2 * pair + 1) * HALF : (2 * pair + 2) * HALF, :] = jnp.where(low_half, turned_q[:HALF], q[HALF:]).astype(BF)
         skv[first : first + MY_ROWS, :] = jnp.where(low, k, turned_v).astype(BF)
         skv[second : second + MY_ROWS, :] = jnp.where(low, turned_k, v).astype(BF)
 
@@ -52,10 +54,10 @@
     nbr, q1, k1, v1, x2, w_view_out, norm_gain, w_qkv, w_out,
     feats_out, lrm_out,
     q_in, k_in, v_in, x_in, gain_in, wv, wqkv, wo,
-    sq_one, skv_one, qb_one, kv_one, so_one, ro_one,
-    sq_two, skv_two, qb_two, kv_two, so_two, ro_two,
-    peak, acc, feats, result,
-    load_sem, weight_sem, out_sem, a2a_send, a2a_q, a2a_kv, ring_send, ring_recv, pair_send, pair_recv, back_send, back_recv,
+    sq_one, skv_one, rq_one, kv_one, so_one, ro_one,
+    sq_two, skv_two, rq_two, kv_two, so_two, ro_two,
+    mask_out, mask_in, qb, scores_a, scores_b, top_a, top_b, peak, acc, feats, result,
+    load_sem, weight_sem, out_sem, a2a_send, a2a_q, a2a_kv, ring_send, ring_recv, pair_send, pair_recv, back_send, back_recv, mask_sem,
 ):
     view = lax.axis_index("view")
     tok = lax.axis_index("tok")
@@ -114,46 +116,50 @@
     low_ones = jnp.where(lane < HD, 1.0, 0.0).astype(BF)
     high_ones = jnp.where(lane < HD, 0.0, 1.0).astype(BF)
 
-    def all_to_all(stage, sq, skv, qb, kv):
-        def send(i, _):
-            head = (my_head + i) % HEADS
-            head_view, head_tok = head_device(head)
-            mine = jnp.logical_and(head_view == view, head_tok == tok)
-            src_q = rows_of(sq, head * MY_ROWS, MY_ROWS)
-            dst_q = rows_of(qb, tok * MY_ROWS, MY_ROWS)
-            src_kv = rows_of(skv, head * MY_ROWS, MY_ROWS)
-            dst_kv = rows_of(kv, view * ROWS + tok * MY_ROWS, MY_ROWS)
-            sem_kv = a2a_kv.at[stage, tok * MY_ROWS // PIECE]
-
-            @pl.when(mine)
-            def _():
-                pltpu.make_async_copy(src_kv, dst_kv, sem_kv).start()
-                pltpu.make_async_copy(src_q, dst_q, a2a_q.at[stage]).start()
-
-            @pl.when(jnp.logical_not(mine))
-            def _():
-                for src, dst, sem, k in ((src_kv, dst_kv, sem_kv, 0), (src_q, dst_q, a2a_q.at[stage], 1)):
+    def all_to_all(stage, sq, skv, rq, kv):
+        def send(src_of, dst, which, sem):
+            def body(i, _):
+                head = (my_head + i) % HEADS
+                head_view, head_tok = head_device(head)
+                mine = jnp.logical_and(head_view == view, head_tok == tok)
+
+                @pl.when(mine)
+                def _():
+                    pltpu.make_async_copy(src_of(head), dst, sem).start()
+
+                @pl.when(jnp.logical_not(mine))
+                def _():
                     pltpu.make_async_remote_copy(
-                        src_ref=src,
+                        src_ref=src_of(head),
                         dst_ref=dst,
-                        send_sem=a2a_send.at[stage, k],
+                        send_sem=a2a_send.at[stage, which],
                         recv_sem=sem,
                         device_id=(head_view, head_tok),
                         device_id_type=MESH,
                     ).start()
 
-            return 0
-
-        lax.fori_loop(0, HEADS, send, 0)
-
-    def sent(like, sem):
+                return 0
+
+            lax.fori_loop(0, HEADS, body, 0)
+
+        send(
+            lambda head: rows_of(skv, head * MY_ROWS, MY_ROWS),
+            rows_of(kv, view * ROWS + tok * MY_ROWS, MY_ROWS),
+            0,
+            a2a_kv.at[stage, tok * MY_ROWS // PIECE],
+        )
+        send(
+            lambda head: rows_of(sq, head * HALF, HALF), rows_of(rq, tok * HALF, HALF), 1, a2a_q.at[stage]
+        )
+
+    def sent(like, rows, sem):
         @pl.when(at_home)
         def _():
-            wait_bytes(like.at[pl.ds(0, (HEADS - 1) * MY_ROWS), :], sem)
+            wait_bytes(like.at[pl.ds(0, (HEADS - 1) * rows), :], sem)
 
         @pl.when(jnp.logical_not(at_home))
         def _():
-            wait_bytes(like.at[pl.ds(0, HEADS * MY_ROWS), :], sem)
+            wait_bytes(like.at[pl.ds(0, HEADS * rows), :], sem)
 
     def ring_piece(stage, kv, direction, step, sub):
         from_z = (z + Z - step) % Z if direction == 0 else (z + step) % Z
@@ -178,29 +184,36 @@
             device_id_type=MESH,
         ).start()
 
-    def absorb(kv, qb, which, masked):
-        block = kv[pl.ds(pl.multiple_of(which * ROWS, ROWS), ROWS), :]
-        keys = block
+    halves = (slice(0, ROWS // 2), slice(ROWS // 2, ROWS))
+
+    def block_of(kv, which):
+        return kv[pl.ds(pl.multiple_of(which * ROWS, ROWS), ROWS), :]
+
+    def score(kv, which, masked, scores, top):
+        keys = block_of(kv, which)
         if masked:
-            hot = jnp.where(lane == HD + which, 1.0, 0.0).astype(BF)
-            keys = block * low_ones + hot
-        values = block * high_ones + low_ones
-        for half in range(2):
-            cols = slice(half * (ROWS // 2), (half + 1) * (ROWS // 2))
-            scores = lax.dot_general(
+            keys = keys * low_ones + jnp.where(lane == HD + which, 1.0, 0.0).astype(BF)
+        for cols in halves:
+            part = lax.dot_general(
                 keys, qb[cols, :], (((1,), (1,)), ((), ())), preferred_element_type=F32
             )
+            scores[:, cols] = part
+            top[:, cols] = jnp.max(part, axis=0, keepdims=True)
+
+    def weigh(kv, which, scores, top):
+        values = block_of(kv, which) * high_ones + low_ones
+        for cols in halves:
             old = peak[:, cols]
-            new = jnp.maximum(old, jnp.max(scores, axis=0, keepdims=True))
+            new = jnp.maximum(old, top[:, cols])
             factor = jnp.exp2((old - new) * EXP2_SCALE)
-            weights16 = jnp.exp2((scores - new) * EXP2_SCALE).astype(BF)
+            weights16 = jnp.exp2((scores[:, cols] - new) * EXP2_SCALE).astype(BF)
             part = lax.dot_general(
                 values, weights16, (((0,), (0,)), ((), ())), preferred_element_type=F32
             )
             acc[:, cols] = acc[:, cols] * factor + part
             peak[:, cols] = new
 
-    def attend(stage, qb, kv, masked):
+    def attend(stage, rq, kv, masked):
         peak[...] = jnp.full_like(peak, START_MAX)
         acc[...] = jnp.zeros_like(acc)
         for sub in range(SUB):
@@ -208,7 +221,11 @@
             ring_piece(stage, kv, 0, 0, sub)
             ring_piece(stage, kv, 1, 0, sub)
             to_partner(stage, kv, z, sub, 0)
-        wait_bytes(qb, a2a_q.at[stage])
+        wait_bytes(rq, a2a_q.at[stage])
+        extra = mask_in[0:1, :].astype(F32) if masked else jnp.zeros((1, LANES), F32)
+        both = rq[...].astype(F32)
+        qb[halves[0], :] = jnp.where(lane < HD, both, extra).astype(BF)
+        qb[halves[1], :] = jnp.where(lane < HD, pltpu.roll(both, HD, 1), extra).astype(BF)
 
         def piece_of(step, sub, direction):
             from_z = (z + Z - step) % Z if direction == 0 else (z + step) % Z
@@ -226,8 +243,7 @@
 
             to_partner(stage, kv, from_z, sub, jnp.minimum(slot, Z - 1))
 
-        def step_of(i, _):
-            step, sub = i // SUB + 1, i % SUB
+        def pieces(step, sub):
             last = step == Z // 2
 
             @pl.when(jnp.logical_or(jnp.logical_not(last), sub < SUB // 2))
@@ -238,39 +254,49 @@
             def _():
                 piece_of(step, sub, 1)
 
-            @pl.when(jnp.logical_or(step > 1, sub < 2))
+        def view_of(chip_z, whose):
+            return chip_z * 2 + core + whose * (1 - 2 * core)
+
+        def from_partner(which, slot):
+            wait_bytes(rows_of(kv, which * ROWS, ROWS), pair_recv.at[stage, slot])
+
+        a, b = (scores_a, top_a), (scores_b, top_b)
+        pieces(1, 0)
+        score(kv, view_of(z, 0), masked, *a)
+        pieces(1, 1)
+        from_partner(view_of(z, 1), 0)
+        score(kv, view_of(z, 1), masked, *b)
+        weigh(kv, view_of(z, 0), *a)
+        pieces(1, 2)
+        pieces(1, 3)
+
+        def two_blocks(i, before):
+            behind, whose = i // 2 + 1, i % 2
+            step = behind + 1
+            right_view = view_of((z + Z - behind) % Z, whose)
+            left_view = view_of((z + behind) % Z, whose)
+            pieces(step, whose * 2)
+
+            @pl.when(whose == 1)
             def _():
-                direction, other = sub % 2, sub // 2
-                first = step == 1
-                behind = step - 1
-                from_z = jnp.where(direction == 0, (z + Z - behind) % Z, (z + behind) % Z)
-                use_other = jnp.where(first, sub, other)
-                whose = core + use_other * (1 - 2 * core)
-                which = jnp.where(first, z, from_z) * 2 + whose
-                slot = jnp.where(first, 0, 2 * behind - 1 + direction)
-
-                @pl.when(use_other == 1)
-                def _():
-                    wait_bytes(rows_of(kv, which * ROWS, ROWS), pair_recv.at[stage, slot])
-
-                absorb(kv, qb, which, masked)
-
-            return 0
-
-        lax.fori_loop(0, Z // 2 * SUB, step_of, 0)
-        far = (z + Z // 2) % Z * 2
-
-        def last_two(i, _):
-            which = far + core + i * (1 - 2 * core)
-
-            @pl.when(i == 1)
-            def _():
-                wait_bytes(rows_of(kv, which * ROWS, ROWS), pair_recv.at[stage, Z - 1])
-
-            absorb(kv, qb, which, masked)
-            return 0
-
-        lax.fori_loop(0, 2, last_two, 0)
+                from_partner(right_view, 2 * behind - 1)
+                from_partner(left_view, 2 * behind)
+
+            score(kv, right_view, masked, *a)
+            weigh(kv, before, *b)
+            pieces(step, whose * 2 + 1)
+            score(kv, left_view, masked, *b)
+            weigh(kv, right_view, *a)
+            return left_view
+
+        before = lax.fori_loop(0, Z - 2, two_blocks, view_of(z, 1))
+        far = (z + Z // 2) % Z
+        score(kv, view_of(far, 0), masked, *a)
+        weigh(kv, before, *b)
+        from_partner(view_of(far, 1), Z - 1)
+        score(kv, view_of(far, 1), masked, *b)
+        weigh(kv, view_of(far, 0), *a)
+        weigh(kv, view_of(far, 1), *b)
 
     def ring_sent(stage, kv):
         for direction in range(2):
@@ -278,14 +304,14 @@
         wait_bytes(kv.at[pl.ds(0, Z * ROWS), :], pair_send.at[stage])
 
     def send_back(stage, so, ro):
-        whole = acc[...]
-        so[...] = jnp.transpose(whole * (1.0 / whole[0:1, :])).astype(BF)
+        first, second = (acc[HD:, cols] * (1.0 / acc[0:1, cols]) for cols in halves)
+        so[...] = jnp.transpose(jnp.concatenate([first, second], axis=0)).astype(BF)
 
         def send(i, _):
             member = (tok + i) % TOKS
             mine = jnp.logical_and(my_view == view, member == tok)
-            src = rows_of(so, member * MY_ROWS, MY_ROWS)
-            dst = rows_of(ro, my_head * MY_ROWS, MY_ROWS)
+            src = rows_of(so, member * HALF, HALF)
+            dst = rows_of(ro, my_head * HALF, HALF)
 
             @pl.when(mine)
             def _():
@@ -308,12 +334,14 @@
         wait_bytes(ro, back_recv.at[stage])
 
     def side_by_side(ro):
-        low = lax.broadcasted_iota(jnp.int32, (MY_ROWS, LANES), 1) < HD
+        low = lax.broadcasted_iota(jnp.int32, (HALF, LANES), 1) < HD
         parts = []
         for pair in range(HEADS // 2):
-            first = ro[2 * pair * MY_ROWS : (2 * pair + 1) * MY_ROWS, :].astype(F32)
-            second = ro[(2 * pair + 1) * MY_ROWS : (2 * pair + 2) * MY_ROWS, :].astype(F32)
-            parts.append(jnp.where(low, pltpu.roll(first, HD, 1), second))
+            first = ro[2 * pair * HALF : (2 * pair + 1) * HALF, :].astype(F32)
+            second = ro[(2 * pair + 1) * HALF : (2 * pair + 2) * HALF, :].astype(F32)
+            early = jnp.where(low, first, pltpu.roll(second, HD, 1))
+            late = jnp.where(low, pltpu.roll(first, HD, 1), second)
+            parts.append(jnp.concatenate([early, late], axis=0))
         return jnp.concatenate(parts, axis=1)
 
     def unit(values):
@@ -321,19 +349,37 @@
 
     for copy in loads[:3]:
         copy.wait()
-    lanes = lax.broadcasted_iota(jnp.int32, (MY_ROWS, LANES), 1)
+    lanes = lax.broadcasted_iota(jnp.int32, mask_out.shape, 1)
     wanted = lanes == HD + view
     for i in range(nbr.shape[1]):
         wanted = jnp.logical_or(wanted, lanes == HD + nbr[0, i])
-    bias = jnp.where(jnp.logical_or(wanted, lanes >= HD + VIEWS), 0.0, NEGATIVE)
+    mask_out[...] = jnp.where(jnp.logical_or(wanted, lanes >= HD + VIEWS), 0.0, NEGATIVE).astype(BF)
 
     def cut(ref):
         return lambda pair: ref[:, pair * LANES : (pair + 1) * LANES].astype(F32)
 
-    pack(cut(q_in), cut(k_in), cut(v_in), bias, sq_one, skv_one)
+    pack(cut(q_in), cut(k_in), cut(v_in), sq_one, skv_one)
     pl.semaphore_wait(barrier, jnp.where(at_home, 2 * TOKS + 1, 2 * TOKS + 3))
-    all_to_all(0, sq_one, skv_one, qb_one, kv_one)
-    attend(0, qb_one, kv_one, True)
+    all_to_all(0, sq_one, skv_one, rq_one, kv_one)
+
+    @pl.when(at_home)
+    def _():
+        pltpu.make_async_copy(mask_out, mask_in, mask_sem.at[1]).start()
+
+    @pl.when(jnp.logical_not(at_home))
+    def _():
+        pltpu.make_async_remote_copy(
+            src_ref=mask_out,
+            dst_ref=mask_in,
+            send_sem=mask_sem.at[0],
+            recv_sem=mask_sem.at[1],
+            device_id=(my_view, tok - core + y_hi),
+            device_id_type=MESH,
+        ).start()
+        wait_bytes(mask_out, mask_sem.at[0])
+
+    wait_bytes(mask_in, mask_sem.at[1])
+    attend(0, rq_one, kv_one, True)
     send_back(0, so_one, ro_one)
 
     attn = side_by_side(ro_one)
@@ -355,10 +401,10 @@
     def cut_value(value):
         return lambda pair: value[:, pair * LANES : (pair + 1) * LANES]
 
-    pack(*(cut_value(part) for part in projected), jnp.zeros((MY_ROWS, LANES), F32), sq_two, skv_two)
-
-    all_to_all(1, sq_two, skv_two, qb_two, kv_two)
-    attend(1, qb_two, kv_two, False)
+    pack(*(cut_value(part) for part in projected), sq_two, skv_two)
+
+    all_to_all(1, sq_two, skv_two, rq_two, kv_two)
+    attend(1, rq_two, kv_two, False)
     send_back(1, so_two, ro_two)
     unit_rows = unit(side_by_side(ro_two)).astype(BF)
     weights[2].wait()
@@ -369,10 +415,10 @@
     for stage, (sq, skv, kv, so) in enumerate(
         ((sq_one, skv_one, kv_one, so_one), (sq_two, skv_two, kv_two, so_two))
     ):
-        sent(skv, a2a_send.at[stage, 0])
-        sent(sq, a2a_send.at[stage, 1])
+        sent(skv, MY_ROWS, a2a_send.at[stage, 0])
+        sent(sq, HALF, a2a_send.at[stage, 1])
         ring_sent(stage, kv)
-        sent(so, back_send.at[stage])
+        sent(so, HALF, back_send.at[stage])
     feats_copy.wait()
     result_copy.wait()
 
@@ -381,12 +427,12 @@
     anywhere = pl.BlockSpec(memory_space=pl.ANY)
     dma = pltpu.SemaphoreType.DMA
     stage_buffers = [
-        pltpu.VMEM((ROWS, LANES), BF),
-        pltpu.VMEM((ROWS, LANES), BF),
-        pltpu.VMEM((ROWS, LANES), BF),
+        pltpu.VMEM((HEADS * HALF, LANES), BF),
+        pltpu.VMEM((HEADS * MY_ROWS, LANES), BF),
+        pltpu.VMEM((TOKS * HALF, LANES), BF),
         pltpu.VMEM((VIEWS * ROWS, LANES), BF),
-        pltpu.VMEM((ROWS, LANES), BF),
-        pltpu.VMEM((ROWS, LANES), BF),
+        pltpu.VMEM((TOKS * HALF, LANES), BF),
+        pltpu.VMEM((HEADS * HALF, LANES), BF),
     ]
     return tuple(pl.pallas_call(
         kernel,
@@ -405,6 +451,13 @@
         ]
         + stage_buffers * 2
         + [
+            pltpu.VMEM((HALF, LANES), BF),
+            pltpu.VMEM((HALF, LANES), BF),
+            pltpu.VMEM((ROWS, LANES), BF),
+            pltpu.VMEM((ROWS, ROWS), F32),
+            pltpu.VMEM((ROWS, ROWS), F32),
+            pltpu.VMEM((1, ROWS), F32),
+            pltpu.VMEM((1, ROWS), F32),
             pltpu.VMEM((1, ROWS), F32),
             pltpu.VMEM((LANES, ROWS), F32),
             pltpu.VMEM((MY_ROWS, WIDTH), F32),
@@ -419,6 +472,7 @@
             dma((2, 2, Z // 2 * SUB)),
             dma((2,)),
             dma((2, Z)),
+            dma((2,)),
             dma((2,)),
             dma((2,)),
         ],

time: 85.7 us -> 73.7 us (0.86)
  Pallas kernels: 81.8 us -> 69.8 us
    pallas_call x1, Pallas kernels: 81.8 us -> 69.8 us  [per_device(): pl.pallas_call(kernel, out_shape=(jax.ShapeDtypeStruct((1, MY_ROWS, WIDTH...]
where the time goes in v2:
time: 73.7 us; the launch traced here: 73.6 us
  Pallas kernels  69.8 us (95%)
  local copies, waits for them, and re-layouts  3.14 us (4%)
    pallas_call x1, Pallas kernels, per_device(): pl.pallas_call(kernel, out_shape=(jax.ShapeDtypeStruct((1, MY_ROWS, WIDTH...  69.8 us
    unnamed x2, local copies, waits for them, and re-layouts  3.14 us

profile of v2, /device:TPU:1, one launch (start us, length us, event | category | flops | bytes accessed | tf_op | source)
XLA Modules:
  0.0 73.6 jit_solution(5756319975143089092)
XLA Ops:
  0.6 69.8 %shard_map.104 = (f32[1,32,1024]{2,1,0:T(8,128)}, f32[1,32,1024]{2,1,0:T(8,128)}) custom-call(s32[1,7]{1,0:T(1,128)} %nbr.1, bf16[1,32,1024]{2,1,0:T(8,128)(2,1)} %q1.1, bf16[1,32,1024]{2,1,0:T(8,128)(2,1)} %k1.1, bf16[1,32,1024]{2,1,0:T(8,128)(2,1)} %v1.1, bf16[1,32,1024]{2,1,0:T(8,128)(2,1)} %x2.1, bf16[1024,1024]{1,0:T(8,128)(2,1)} %w_view_out.1, ...), custom_call_target="tpu_custom_call" | custom-call | tf_op jit(solution)/shard_map/pallas_call | solution.py:437
  70.5 1.6 %copy.13 = f32[1,32,1024]{2,1,0:T(8,128)} copy(f32[1,32,1024]{2,1,0:T(8,128)} %get-tuple-element.4) | data formatting | bytes 262144
  72.0 1.6 %copy.14 = f32[1,32,1024]{2,1,0:T(8,128)} copy(f32[1,32,1024]{2,1,0:T(8,128)} %get-tuple-element.5) | data formatting | bytes 262144

commit v3 on v2

--- a/solution.py
+++ b/solution.py
@@ -37,23 +37,28 @@
     return ref.at[pl.ds(pl.multiple_of(start, count if count < 128 else 128), count), :]
 
 
-def pack(q_of, k_of, v_of, sq, skv):
+def pack_keys(k_of, v_of, skv):
     low = lax.broadcasted_iota(jnp.int32, (MY_ROWS, LANES), 1) < HD
-    low_half = lax.broadcasted_iota(jnp.int32, (HALF, LANES), 1) < HD
     for pair in range(HEADS // 2):
-        q, k, v = q_of(pair), k_of(pair), v_of(pair)
-        turned_q, turned_k, turned_v = (pltpu.roll(part, HD, 1) for part in (q, k, v))
+        k, v = k_of(pair), v_of(pair)
         first, second = 2 * pair * MY_ROWS, (2 * pair + 1) * MY_ROWS
-        sq[2 * pair * HALF : (2 * pair + 1) * HALF, :] = jnp.where(low_half, q[:HALF], turned_q[HALF:]).astype(BF)
-        sq[(2 * pair + 1) * HALF : (2 * pair + 2) * HALF, :] = jnp.where(low_half, turned_q[:HALF], q[HALF:]).astype(BF)
-        skv[first : first + MY_ROWS, :] = jnp.where(low, k, turned_v).astype(BF)
-        skv[second : second + MY_ROWS, :] = jnp.where(low, turned_k, v).astype(BF)
+        skv[first : first + MY_ROWS, :] = jnp.where(low, k, pltpu.roll(v, HD, 1)).astype(BF)
+        skv[second : second + MY_ROWS, :] = jnp.where(low, pltpu.roll(k, HD, 1), v).astype(BF)
+
+
+def pack_queries(q_of, sq):
+    low = lax.broadcasted_iota(jnp.int32, (HALF, LANES), 1) < HD
+    for pair in range(HEADS // 2):
+        q = q_of(pair)
+        turned = pltpu.roll(q, HD, 1)
+        sq[2 * pair * HALF : (2 * pair + 1) * HALF, :] = jnp.where(low, q[:HALF], turned[HALF:]).astype(BF)
+        sq[(2 * pair + 1) * HALF : (2 * pair + 2) * HALF, :] = jnp.where(low, turned[:HALF], q[HALF:]).astype(BF)
 
 
 def kernel(
-    nbr, q1, k1, v1, x2, w_view_out, norm_gain, w_qkv, w_out,
+    nbr_hbm, q1, k1, v1, x2, w_view_out, norm_gain, w_qkv, w_out,
     feats_out, lrm_out,
-    q_in, k_in, v_in, x_in, gain_in, wv, wqkv, wo,
+    nbr, q_in, k_in, v_in, x_in, gain_in, wv, wqkv, wo,
     sq_one, skv_one, rq_one, kv_one, so_one, ro_one,
     sq_two, skv_two, rq_two, kv_two, so_two, ro_two,
     mask_out, mask_in, qb, scores_a, scores_b, top_a, top_b, peak, acc, feats, result,
@@ -73,7 +78,7 @@
     loads = [
         pltpu.make_async_copy(src, dst, load_sem.at[i])
         for i, (src, dst) in enumerate(
-            ((q1.at[0], q_in), (k1.at[0], k_in), (v1.at[0], v_in), (x2.at[0], x_in), (norm_gain, gain_in))
+            ((k1.at[0], k_in), (v1.at[0], v_in), (q1.at[0], q_in), (nbr_hbm, nbr), (x2.at[0], x_in), (norm_gain, gain_in))
         )
     ]
     weights = [
@@ -116,40 +121,50 @@
     low_ones = jnp.where(lane < HD, 1.0, 0.0).astype(BF)
     high_ones = jnp.where(lane < HD, 0.0, 1.0).astype(BF)
 
-    def all_to_all(stage, sq, skv, rq, kv):
-        def send(src_of, dst, which, sem):
-            def body(i, _):
-                head = (my_head + i) % HEADS
-                head_view, head_tok = head_device(head)
-                mine = jnp.logical_and(head_view == view, head_tok == tok)
-
-                @pl.when(mine)
-                def _():
-                    pltpu.make_async_copy(src_of(head), dst, sem).start()
-
-                @pl.when(jnp.logical_not(mine))
-                def _():
-                    pltpu.make_async_remote_copy(
-                        src_ref=src_of(head),
-                        dst_ref=dst,
-                        send_sem=a2a_send.at[stage, which],
-                        recv_sem=sem,
-                        device_id=(head_view, head_tok),
-                        device_id_type=MESH,
-                    ).start()
-
-                return 0
-
-            lax.fori_loop(0, HEADS, body, 0)
-
-        send(
-            lambda head: rows_of(skv, head * MY_ROWS, MY_ROWS),
+    def spread(src_of, dst, device_of, send_sem, recv_sem):
+        def remote(i):
+            pltpu.make_async_remote_copy(
+                src_ref=src_of(i),
+                dst_ref=dst,
+                send_sem=send_sem,
+                recv_sem=recv_sem,
+                device_id=device_of(i),
+                device_id_type=MESH,
+            ).start()
+
+        def body(i, _):
+            remote(i)
+            return 0
+
+        lax.fori_loop(1, TOKS, body, 0)
+
+        @pl.when(at_home)
+        def _():
+            pltpu.make_async_copy(src_of(0), dst, recv_sem).start()
+
+        @pl.when(jnp.logical_not(at_home))
+        def _():
+            remote(0)
+
+    def nth_head(i):
+        return (my_head + i) % HEADS
+
+    def send_keys(stage, skv, kv):
+        spread(
+            lambda i: rows_of(skv, nth_head(i) * MY_ROWS, MY_ROWS),
             rows_of(kv, view * ROWS + tok * MY_ROWS, MY_ROWS),
-            0,
+            lambda i: head_device(nth_head(i)),
+            a2a_send.at[stage, 0],
             a2a_kv.at[stage, tok * MY_ROWS // PIECE],
         )
-        send(
-            lambda head: rows_of(sq, head * HALF, HALF), rows_of(rq, tok * HALF, HALF), 1, a2a_q.at[stage]
+
+    def send_queries(stage, sq, rq):
+        spread(
+            lambda i: rows_of(sq, nth_head(i) * HALF, HALF),
+            rows_of(rq, tok * HALF, HALF),
+            lambda i: head_device(nth_head(i)),
+            a2a_send.at[stage, 1],
+            a2a_q.at[stage],
         )
 
     def sent(like, rows, sem):
@@ -220,8 +235,11 @@
             wait_bytes(rows_of(kv, my_view * ROWS + sub * PIECE, PIECE), a2a_kv.at[stage, sub])
             ring_piece(stage, kv, 0, 0, sub)
             ring_piece(stage, kv, 1, 0, sub)
+        for sub in range(SUB):
             to_partner(stage, kv, z, sub, 0)
         wait_bytes(rq, a2a_q.at[stage])
+        if masked:
+            wait_bytes(mask_in, mask_sem.at[1])
         extra = mask_in[0:1, :].astype(F32) if masked else jnp.zeros((1, LANES), F32)
         both = rq[...].astype(F32)
         qb[halves[0], :] = jnp.where(lane < HD, both, extra).astype(BF)
@@ -229,30 +247,29 @@
 
         def piece_of(step, sub, direction):
             from_z = (z + Z - step) % Z if direction == 0 else (z + step) % Z
-            slot = 2 * step - 1 + direction
             block = rows_of(kv, (from_z * 2 + core) * ROWS + sub * PIECE, PIECE)
             wait_bytes(block, ring_recv.at[stage, direction, (step - 1) * SUB + sub])
-            if direction == 0:
-                go_on = jnp.logical_or(step < Z // 2 - 1, sub < SUB // 2)
-            else:
-                go_on = jnp.logical_or(step < Z // 2 - 1, sub >= SUB // 2)
-
-            @pl.when(jnp.logical_and(step < Z // 2, go_on))
+            return from_z
+
+        def pieces(step, sub):
+            right_z = piece_of(step, sub, 0)
+
+            @pl.when(jnp.logical_or(step < Z // 2 - 1, sub < SUB // 2))
             def _():
-                ring_piece(stage, kv, direction, step, sub)
-
-            to_partner(stage, kv, from_z, sub, jnp.minimum(slot, Z - 1))
-
-        def pieces(step, sub):
-            last = step == Z // 2
-
-            @pl.when(jnp.logical_or(jnp.logical_not(last), sub < SUB // 2))
+                ring_piece(stage, kv, 0, step, sub)
+
+            left_z = piece_of(step, sub, 1)
+
+            @pl.when(jnp.logical_or(step < Z // 2 - 1, sub >= SUB // 2))
             def _():
-                piece_of(step, sub, 0)
-
-            @pl.when(jnp.logical_or(jnp.logical_not(last), sub >= SUB // 2))
-            def _():
-                piece_of(step, sub, 1)
+                ring_piece(stage, kv, 1, step, sub)
+
+            to_partner(stage, kv, right_z, sub, 2 * step - 1)
+            to_partner(stage, kv, left_z, sub, 2 * step)
+
+        def last_pieces(sub):
+            for direction, piece in ((0, sub), (1, SUB // 2 + sub)):
+                to_partner(stage, kv, piece_of(Z // 2, piece, direction), piece, Z - 1)
 
         def view_of(chip_z, whose):
             return chip_z * 2 + core + whose * (1 - 2 * core)
@@ -270,12 +287,10 @@
         pieces(1, 2)
         pieces(1, 3)
 
-        def two_blocks(i, before):
-            behind, whose = i // 2 + 1, i % 2
-            step = behind + 1
+        def two_blocks(behind, whose, before, ahead):
             right_view = view_of((z + Z - behind) % Z, whose)
             left_view = view_of((z + behind) % Z, whose)
-            pieces(step, whose * 2)
+            ahead(0)
 
             @pl.when(whose == 1)
             def _():
@@ -284,18 +299,29 @@
 
             score(kv, right_view, masked, *a)
             weigh(kv, before, *b)
-            pieces(step, whose * 2 + 1)
+            ahead(1)
             score(kv, left_view, masked, *b)
             weigh(kv, right_view, *a)
             return left_view
 
-        before = lax.fori_loop(0, Z - 2, two_blocks, view_of(z, 1))
+        def middle(i, before):
+            behind, whose = i // 2 + 1, i % 2
+            return two_blocks(behind, whose, before, lambda j: pieces(behind + 1, whose * 2 + j))
+
+        before = lax.fori_loop(0, Z - 4, middle, view_of(z, 1))
         far = (z + Z // 2) % Z
+
+        def final(whose, before):
+            return two_blocks(Z // 2 - 1, whose, before, lambda j: None)
+
+        before = lax.fori_loop(0, 2, final, before)
+        weigh(kv, before, *b)
+        last_pieces(0)
+        last_pieces(1)
         score(kv, view_of(far, 0), masked, *a)
-        weigh(kv, before, *b)
+        weigh(kv, view_of(far, 0), *a)
         from_partner(view_of(far, 1), Z - 1)
         score(kv, view_of(far, 1), masked, *b)
-        weigh(kv, view_of(far, 0), *a)
         weigh(kv, view_of(far, 1), *b)
 
     def ring_sent(stage, kv):
@@ -307,30 +333,13 @@
         first, second = (acc[HD:, cols] * (1.0 / acc[0:1, cols]) for cols in halves)
         so[...] = jnp.transpose(jnp.concatenate([first, second], axis=0)).astype(BF)
 
-        def send(i, _):
-            member = (tok + i) % TOKS
-            mine = jnp.logical_and(my_view == view, member == tok)
-            src = rows_of(so, member * HALF, HALF)
-            dst = rows_of(ro, my_head * HALF, HALF)
-
-            @pl.when(mine)
-            def _():
-                pltpu.make_async_copy(src, dst, back_recv.at[stage]).start()
-
-            @pl.when(jnp.logical_not(mine))
-            def _():
-                pltpu.make_async_remote_copy(
-                    src_ref=src,
-                    dst_ref=dst,
-                    send_sem=back_send.at[stage],
-                    recv_sem=back_recv.at[stage],
-                    device_id=(my_view, member),
-                    device_id_type=MESH,
-                ).start()
-
-            return 0
-
-        lax.fori_loop(0, TOKS, send, 0)
+        spread(
+            lambda i: rows_of(so, (tok + i) % TOKS * HALF, HALF),
+            rows_of(ro, my_head * HALF, HALF),
+            lambda i: (my_view, (tok + i) % TOKS),
+            back_send.at[stage],
+            back_recv.at[stage],
+        )
         wait_bytes(ro, back_recv.at[stage])
 
     def side_by_side(ro):
@@ -347,20 +356,24 @@
     def unit(values):
         return values * lax.rsqrt(jnp.mean(values * values, axis=-1, keepdims=True) + EPSILON)
 
-    for copy in loads[:3]:
+    for copy in loads[:2]:
         copy.wait()
+
+    def cut(ref):
+        return lambda pair: ref[:, pair * LANES : (pair + 1) * LANES].astype(F32)
+
+    pack_keys(cut(k_in), cut(v_in), skv_one)
+    pl.semaphore_wait(barrier, jnp.where(at_home, 2 * TOKS + 1, 2 * TOKS + 3))
+    send_keys(0, skv_one, kv_one)
+    for copy in loads[2:4]:
+        copy.wait()
+    pack_queries(cut(q_in), sq_one)
+    send_queries(0, sq_one, rq_one)
     lanes = lax.broadcasted_iota(jnp.int32, mask_out.shape, 1)
     wanted = lanes == HD + view
     for i in range(nbr.shape[1]):
         wanted = jnp.logical_or(wanted, lanes == HD + nbr[0, i])
     mask_out[...] = jnp.where(jnp.logical_or(wanted, lanes >= HD + VIEWS), 0.0, NEGATIVE).astype(BF)
-
-    def cut(ref):
-        return lambda pair: ref[:, pair * LANES : (pair + 1) * LANES].astype(F32)
-
-    pack(cut(q_in), cut(k_in), cut(v_in), sq_one, skv_one)
-    pl.semaphore_wait(barrier, jnp.where(at_home, 2 * TOKS + 1, 2 * TOKS + 3))
-    all_to_all(0, sq_one, skv_one, rq_one, kv_one)
 
     @pl.when(at_home)
     def _():
@@ -376,41 +389,36 @@
             device_id=(my_view, tok - core + y_hi),
             device_id_type=MESH,
         ).start()
-        wait_bytes(mask_out, mask_sem.at[0])
-
-    wait_bytes(mask_in, mask_sem.at[1])
+
     attend(0, rq_one, kv_one, True)
     send_back(0, so_one, ro_one)
 
     attn = side_by_side(ro_one)
     feats_f32 = unit(attn)
-    feats[...] = feats_f32
-    feats_copy = pltpu.make_async_copy(feats, feats_out.at[0], out_sem.at[0])
-    feats_copy.start()
-    for copy in loads[3:]:
+    feats_out[0] = feats_f32
+    for copy in loads[4:]:
         copy.wait()
     weights[0].wait()
     hidden = x_in[...].astype(F32) + jnp.dot(feats_f32.astype(BF), wv[...], preferred_element_type=F32)
     normed = (unit(hidden) * gain_in[...]).astype(BF)
     weights[1].wait()
-    projected = [
-        jnp.dot(normed, wqkv[:, part * WIDTH : (part + 1) * WIDTH], preferred_element_type=F32)
-        for part in range(3)
-    ]
+
+    def project(part):
+        return jnp.dot(normed, wqkv[:, part * WIDTH : (part + 1) * WIDTH], preferred_element_type=F32)
 
     def cut_value(value):
         return lambda pair: value[:, pair * LANES : (pair + 1) * LANES]
 
-    pack(*(cut_value(part) for part in projected), sq_two, skv_two)
-
-    all_to_all(1, sq_two, skv_two, rq_two, kv_two)
+    pack_keys(cut_value(project(1)), cut_value(project(2)), skv_two)
+    send_keys(1, skv_two, kv_two)
+    pack_queries(cut_value(project(0)), sq_two)
+    send_queries(1, sq_two, rq_two)
+
     attend(1, rq_two, kv_two, False)
     send_back(1, so_two, ro_two)
     unit_rows = unit(side_by_side(ro_two)).astype(BF)
     weights[2].wait()
-    result[...] = jnp.dot(unit_rows, wo[...], preferred_element_type=F32)
-    result_copy = pltpu.make_async_copy(result, lrm_out.at[0], out_sem.at[1])
-    result_copy.start()
+    lrm_out[0] = jnp.dot(unit_rows, wo[...], preferred_element_type=F32)
 
     for stage, (sq, skv, kv, so) in enumerate(
         ((sq_one, skv_one, kv_one, so_one), (sq_two, skv_two, kv_two, so_two))
@@ -419,8 +427,10 @@
         sent(sq, HALF, a2a_send.at[stage, 1])
         ring_sent(stage, kv)
         sent(so, HALF, back_send.at[stage])
-    feats_copy.wait()
-    result_copy.wait()
+
+    @pl.when(jnp.logical_not(at_home))
+    def _():
+        wait_bytes(mask_out, mask_sem.at[0])
 
 
 def per_device(q1, k1, v1, nbr, x2, w_view_out, norm_gain, w_qkv, w_out):
@@ -437,12 +447,13 @@
     return tuple(pl.pallas_call(
         kernel,
         out_shape=(
-            jax.ShapeDtypeStruct((1, MY_ROWS, WIDTH), F32),
-            jax.ShapeDtypeStruct((1, MY_ROWS, WIDTH), F32),
+            pltpu.VMEM((1, MY_ROWS, WIDTH), F32),
+            pltpu.VMEM((1, MY_ROWS, WIDTH), F32),
         ),
-        in_specs=[pl.BlockSpec(memory_space=pltpu.SMEM)] + [anywhere] * 8,
-        out_specs=(anywhere, anywhere),
-        scratch_shapes=[pltpu.VMEM((MY_ROWS, WIDTH), BF)] * 4
+        in_specs=[anywhere] * 9,
+        out_specs=(pl.BlockSpec(memory_space=pltpu.VMEM),) * 2,
+        scratch_shapes=[pltpu.SMEM((1, 7), jnp.int32)]
+        + [pltpu.VMEM((MY_ROWS, WIDTH), BF)] * 4
         + [
             pltpu.VMEM((1, WIDTH), F32),
             pltpu.VMEM((WIDTH, WIDTH), BF),
@@ -462,7 +473,7 @@
             pltpu.VMEM((LANES, ROWS), F32),
             pltpu.VMEM((MY_ROWS, WIDTH), F32),
             pltpu.VMEM((MY_ROWS, WIDTH), F32),
-            dma((5,)),
+            dma((6,)),
             dma((3,)),
             dma((2,)),
             dma((2, 2)),

time: 73.7 us -> 70 us (0.950)
  Pallas kernels: 69.8 us -> 67.9 us
  local copies, waits for them, and re-layouts: 3.14 us -> 1.31 us
    pallas_call x1, Pallas kernels: 69.8 us -> 67.9 us  [per_device(): pl.pallas_call(kernel, out_shape=(pltpu.VMEM((1, MY_ROWS, WIDTH), F32), p...]
    unnamed x2, local copies, waits for them, and re-layouts: 3.14 us -> 1.31 us
where the time goes in v3:
time: 70 us; the launch traced here: 69.8 us
  Pallas kernels  67.9 us (97%)
  local copies, waits for them, and re-layouts  1.31 us (2%)
    pallas_call x1, Pallas kernels, per_device(): pl.pallas_call(kernel, out_shape=(pltpu.VMEM((1, MY_ROWS, WIDTH), F32), p...  67.9 us

profile of v3, /device:TPU:1, one launch (start us, length us, event | category | flops | bytes accessed | tf_op | source)
XLA Modules:
  0.0 69.8 jit_solution(14168572430014363755)
XLA Ops:
  0.6 67.9 %shard_map.104 = (f32[1,32,1024]{2,1,0:T(8,128)S(1)}, f32[1,32,1024]{2,1,0:T(8,128)S(1)}) custom-call(s32[1,7]{1,0:T(1,128)} %nbr_hbm.1, bf16[1,32,1024]{2,1,0:T(8,128)(2,1)} %q1.1, bf16[1,32,1024]{2,1,0:T(8,128)(2,1)} %k1.1, bf16[1,32,1024]{2,1,0:T(8,128)(2,1)} %v1.1, bf16[1,32,1024]{2,1,0:T(8,128)(2,1)} %x2.1, bf16[1024,1024]{1,0:T(8,128)(2,1)} %w_view_out.1, ...), custom_call_target="tpu_custom_call" | custom-call | tf_op jit(solution)/shard_map/pallas_call | solution.py:447
  68.5 0.7 copy.13
  69.2 0.7 copy.14

commit v4 on v3

--- a/solution.py
+++ b/solution.py
@@ -29,6 +29,19 @@
 EXP2_SCALE = HD ** (-0.5) * math.log2(math.e)
 
 
+def ring_distance(offset):
+    return min(offset % 4, -offset % 4)
+
+
+CHIP_ORDER = sorted(
+    ((dx, dy) for dy in range(4) for dx in range(4)), key=lambda at: -ring_distance(at[0]) - ring_distance(at[1])
+)
+MEMBER_ORDER = sorted(
+    ((dx, dy, dc) for dy in range(2) for dx in range(4) for dc in range(2)),
+    key=lambda at: (-ring_distance(at[0]), -at[1], -at[2]),
+)
+
+
 def wait_bytes(like, sem):
     pltpu.make_async_copy(like, like, sem).wait()
 
@@ -59,16 +72,17 @@
     nbr_hbm, q1, k1, v1, x2, w_view_out, norm_gain, w_qkv, w_out,
     feats_out, lrm_out,
     nbr, q_in, k_in, v_in, x_in, gain_in, wv, wqkv, wo,
-    sq_one, skv_one, rq_one, kv_one, so_one, ro_one,
-    sq_two, skv_two, rq_two, kv_two, so_two, ro_two,
-    mask_out, mask_in, qb, scores_a, scores_b, top_a, top_b, peak, acc, feats, result,
-    load_sem, weight_sem, out_sem, a2a_send, a2a_q, a2a_kv, ring_send, ring_recv, pair_send, pair_recv, back_send, back_recv, mask_sem,
+    sqs, skvs, rqs, kvs, sos, ros,
+    normed, mask_out, mask_in, qb, scores_a, scores_b, top_a, top_b, peak, acc,
+    load_sem, weight_sem, a2a_send, a2a_q, a2a_kv, ring_send, ring_recv, pair_send, pair_recv, back_send, back_recv, mask_sem,
 ):
     view = lax.axis_index("view")
     tok = lax.axis_index("tok")
     z, y_hi = view // 2, view % 2
     core = tok % 2
-    my_head = y_hi * 8 + tok // 8 * 4 + tok // 2 % 4
+    x, y_lo = tok // 2 % 4, tok // 8
+    y = y_hi * 2 + y_lo
+    my_head = y * 4 + x
     my_view = z * 2 + core
     at_home = core == y_hi
     right = (z + 1) % Z * 2 + y_hi
@@ -132,22 +146,24 @@
                 device_id_type=MESH,
             ).start()
 
-        def body(i, _):
+        for i in range(TOKS - 1):
             remote(i)
-            return 0
-
-        lax.fori_loop(1, TOKS, body, 0)
 
         @pl.when(at_home)
         def _():
-            pltpu.make_async_copy(src_of(0), dst, recv_sem).start()
+            pltpu.make_async_copy(src_of(TOKS - 1), dst, recv_sem).start()
 
         @pl.when(jnp.logical_not(at_home))
         def _():
-            remote(0)
+            remote(TOKS - 1)
 
     def nth_head(i):
-        return (my_head + i) % HEADS
+        dx, dy = CHIP_ORDER[i]
+        return (y + dy) % 4 * 4 + (x + dx) % 4
+
+    def nth_member(i):
+        dx, dy, dc = MEMBER_ORDER[i]
+        return (y_lo + dy) % 2 * 8 + (x + dx) % 4 * 2 + (core + dc) % 2
 
     def send_keys(stage, skv, kv):
         spread(
@@ -204,10 +220,8 @@
     def block_of(kv, which):
         return kv[pl.ds(pl.multiple_of(which * ROWS, ROWS), ROWS), :]
 
-    def score(kv, which, masked, scores, top):
-        keys = block_of(kv, which)
-        if masked:
-            keys = keys * low_ones + jnp.where(lane == HD + which, 1.0, 0.0).astype(BF)
+    def score(kv, which, scores, top):
+        keys = block_of(kv, which) * low_ones + jnp.where(lane == HD + which, 1.0, 0.0).astype(BF)
         for cols in halves:
             part = lax.dot_general(
                 keys, qb[cols, :], (((1,), (1,)), ((), ())), preferred_element_type=F32
@@ -228,7 +242,7 @@
             acc[:, cols] = acc[:, cols] * factor + part
             peak[:, cols] = new
 
-    def attend(stage, rq, kv, masked):
+    def attend(stage, rq, kv):
         peak[...] = jnp.full_like(peak, START_MAX)
         acc[...] = jnp.zeros_like(acc)
         for sub in range(SUB):
@@ -238,9 +252,12 @@
         for sub in range(SUB):
             to_partner(stage, kv, z, sub, 0)
         wait_bytes(rq, a2a_q.at[stage])
-        if masked:
+
+        @pl.when(stage == 0)
+        def _():
             wait_bytes(mask_in, mask_sem.at[1])
-        extra = mask_in[0:1, :].astype(F32) if masked else jnp.zeros((1, LANES), F32)
+
+        extra = jnp.where(stage == 0, mask_in[0:1, :].astype(F32), 0.0)
         both = rq[...].astype(F32)
         qb[halves[0], :] = jnp.where(lane < HD, both, extra).astype(BF)
         qb[halves[1], :] = jnp.where(lane < HD, pltpu.roll(both, HD, 1), extra).astype(BF)
@@ -279,10 +296,10 @@
 
         a, b = (scores_a, top_a), (scores_b, top_b)
         pieces(1, 0)
-        score(kv, view_of(z, 0), masked, *a)
+        score(kv, view_of(z, 0), *a)
         pieces(1, 1)
         from_partner(view_of(z, 1), 0)
-        score(kv, view_of(z, 1), masked, *b)
+        score(kv, view_of(z, 1), *b)
         weigh(kv, view_of(z, 0), *a)
         pieces(1, 2)
         pieces(1, 3)
@@ -297,10 +314,10 @@
                 from_partner(right_view, 2 * behind - 1)
                 from_partner(left_view, 2 * behind)
 
-            score(kv, right_view, masked, *a)
+            score(kv, right_view, *a)
             weigh(kv, before, *b)
             ahead(1)
-            score(kv, left_view, masked, *b)
+            score(kv, left_view, *b)
             weigh(kv, right_view, *a)
             return left_view
 
@@ -318,10 +335,10 @@
         weigh(kv, before, *b)
         last_pieces(0)
         last_pieces(1)
-        score(kv, view_of(far, 0), masked, *a)
+        score(kv, view_of(far, 0), *a)
         weigh(kv, view_of(far, 0), *a)
         from_partner(view_of(far, 1), Z - 1)
-        score(kv, view_of(far, 1), masked, *b)
+        score(kv, view_of(far, 1), *b)
         weigh(kv, view_of(far, 1), *b)
 
     def ring_sent(stage, kv):
@@ -334,9 +351,9 @@
         so[...] = jnp.transpose(jnp.concatenate([first, second], axis=0)).astype(BF)
 
         spread(
-            lambda i: rows_of(so, (tok + i) % TOKS * HALF, HALF),
+            lambda i: rows_of(so, nth_member(i) * HALF, HALF),
             rows_of(ro, my_head * HALF, HALF),
-            lambda i: (my_view, (tok + i) % TOKS),
+            lambda i: (my_view, nth_member(i)),
             back_send.at[stage],
             back_recv.at[stage],
         )
@@ -356,77 +373,89 @@
     def unit(values):
         return values * lax.rsqrt(jnp.mean(values * values, axis=-1, keepdims=True) + EPSILON)
 
+    def cut(ref):
+        return lambda pair: ref[:, pair * LANES : (pair + 1) * LANES].astype(F32)
+
+    def cut_value(value):
+        return lambda pair: value[:, pair * LANES : (pair + 1) * LANES]
+
+    def project(part):
+        return jnp.dot(
+            normed[...], wqkv[:, part * WIDTH : (part + 1) * WIDTH], preferred_element_type=F32
+        )
+
     for copy in loads[:2]:
         copy.wait()
-
-    def cut(ref):
-        return lambda pair: ref[:, pair * LANES : (pair + 1) * LANES].astype(F32)
-
-    pack_keys(cut(k_in), cut(v_in), skv_one)
+    pack_keys(cut(k_in), cut(v_in), skvs.at[0])
     pl.semaphore_wait(barrier, jnp.where(at_home, 2 * TOKS + 1, 2 * TOKS + 3))
-    send_keys(0, skv_one, kv_one)
-    for copy in loads[2:4]:
-        copy.wait()
-    pack_queries(cut(q_in), sq_one)
-    send_queries(0, sq_one, rq_one)
-    lanes = lax.broadcasted_iota(jnp.int32, mask_out.shape, 1)
-    wanted = lanes == HD + view
-    for i in range(nbr.shape[1]):
-        wanted = jnp.logical_or(wanted, lanes == HD + nbr[0, i])
-    mask_out[...] = jnp.where(jnp.logical_or(wanted, lanes >= HD + VIEWS), 0.0, NEGATIVE).astype(BF)
-
-    @pl.when(at_home)
-    def _():
-        pltpu.make_async_copy(mask_out, mask_in, mask_sem.at[1]).start()
-
-    @pl.when(jnp.logical_not(at_home))
-    def _():
-        pltpu.make_async_remote_copy(
-            src_ref=mask_out,
-            dst_ref=mask_in,
-            send_sem=mask_sem.at[0],
-            recv_sem=mask_sem.at[1],
-            device_id=(my_view, tok - core + y_hi),
-            device_id_type=MESH,
-        ).start()
-
-    attend(0, rq_one, kv_one, True)
-    send_back(0, so_one, ro_one)
-
-    attn = side_by_side(ro_one)
-    feats_f32 = unit(attn)
-    feats_out[0] = feats_f32
-    for copy in loads[4:]:
-        copy.wait()
-    weights[0].wait()
-    hidden = x_in[...].astype(F32) + jnp.dot(feats_f32.astype(BF), wv[...], preferred_element_type=F32)
-    normed = (unit(hidden) * gain_in[...]).astype(BF)
-    weights[1].wait()
-
-    def project(part):
-        return jnp.dot(normed, wqkv[:, part * WIDTH : (part + 1) * WIDTH], preferred_element_type=F32)
-
-    def cut_value(value):
-        return lambda pair: value[:, pair * LANES : (pair + 1) * LANES]
-
-    pack_keys(cut_value(project(1)), cut_value(project(2)), skv_two)
-    send_keys(1, skv_two, kv_two)
-    pack_queries(cut_value(project(0)), sq_two)
-    send_queries(1, sq_two, rq_two)
-
-    attend(1, rq_two, kv_two, False)
-    send_back(1, so_two, ro_two)
-    unit_rows = unit(side_by_side(ro_two)).astype(BF)
-    weights[2].wait()
-    lrm_out[0] = jnp.dot(unit_rows, wo[...], preferred_element_type=F32)
-
-    for stage, (sq, skv, kv, so) in enumerate(
-        ((sq_one, skv_one, kv_one, so_one), (sq_two, skv_two, kv_two, so_two))
-    ):
-        sent(skv, MY_ROWS, a2a_send.at[stage, 0])
-        sent(sq, HALF, a2a_send.at[stage, 1])
-        ring_sent(stage, kv)
-        sent(so, HALF, back_send.at[stage])
+
+    def attention(stage, _):
+        sq, skv, rq, kv, so, ro = (ref.at[stage] for ref in (sqs, skvs, rqs, kvs, sos, ros))
+        send_keys(stage, skv, kv)
+
+        @pl.when(stage == 0)
+        def _():
+            for copy in loads[2:4]:
+                copy.wait()
+            pack_queries(cut(q_in), sq)
+            lanes = lax.broadcasted_iota(jnp.int32, mask_out.shape, 1)
+            wanted = lanes == HD + view
+            for i in range(nbr.shape[1]):
+                wanted = jnp.logical_or(wanted, lanes == HD + nbr[0, i])
+            mask_out[...] = jnp.where(jnp.logical_or(wanted, lanes >= HD + VIEWS), 0.0, NEGATIVE).astype(BF)
+
+            @pl.when(at_home)
+            def _():
+                pltpu.make_async_copy(mask_out, mask_in, mask_sem.at[1]).start()
+
+            @pl.when(jnp.logical_not(at_home))
+            def _():
+                pltpu.make_async_remote_copy(
+                    src_ref=mask_out,
+                    dst_ref=mask_in,
+                    send_sem=mask_sem.at[0],
+                    recv_sem=mask_sem.at[1],
+                    device_id=(my_view, tok - core + y_hi),
+                    device_id_type=MESH,
+                ).start()
+
+        @pl.when(stage == 1)
+        def _():
+            pack_queries(cut_value(project(0)), sq)
+
+        send_queries(stage, sq, rq)
+        attend(stage, rq, kv)
+        send_back(stage, so, ro)
+        rows = unit(side_by_side(ro))
+
+        @pl.when(stage == 0)
+        def _():
+            feats_out[0] = rows
+            for copy in loads[4:]:
+                copy.wait()
+            weights[0].wait()
+            hidden = x_in[...].astype(F32) + jnp.dot(rows.astype(BF), wv[...], preferred_element_type=F32)
+            normed[...] = (unit(hidden) * gain_in[...]).astype(BF)
+            weights[1].wait()
+            pack_keys(cut_value(project(1)), cut_value(project(2)), skvs.at[1])
+
+        @pl.when(stage == 1)
+        def _():
+            weights[2].wait()
+            lrm_out[0] = jnp.dot(rows.astype(BF), wo[...], preferred_element_type=F32)
+
+        return 0
+
+    lax.fori_loop(0, 2, attention, 0)
+
+    def finish(stage, _):
+        sent(skvs.at[stage], MY_ROWS, a2a_send.at[stage, 0])
+        sent(sqs.at[stage], HALF, a2a_send.at[stage, 1])
+        ring_sent(stage, kvs.at[stage])
+        sent(sos.at[stage], HALF, back_send.at[stage])
+        return 0
+
+    lax.fori_loop(0, 2, finish, 0)
 
     @pl.when(jnp.logical_not(at_home))
     def _():
@@ -437,12 +466,13 @@
     anywhere = pl.BlockSpec(memory_space=pl.ANY)
     dma = pltpu.SemaphoreType.DMA
     stage_buffers = [
-        pltpu.VMEM((HEADS * HALF, LANES), BF),
-        pltpu.VMEM((HEADS * MY_ROWS, LANES), BF),
-        pltpu.VMEM((TOKS * HALF, LANES), BF),
-        pltpu.VMEM((VIEWS * ROWS, LANES), BF),
-        pltpu.VMEM((TOKS * HALF, LANES), BF),
-        pltpu.VMEM((HEADS * HALF, LANES), BF),
+        pltpu.VMEM((2, HEADS * HALF, LANES), BF),
+        pltpu.VMEM((2, HEADS * MY_ROWS, LANES), BF),
+        pltpu.VMEM((2, TOKS * HALF, LANES), BF),
+        pltpu.VMEM((2, VIEWS * ROWS, LANES), BF),
+        pltpu.VMEM((2, TOKS * HALF, LANES), BF),
+        pltpu.VMEM((2, HEADS * HALF, LANES), BF),
+        pltpu.VMEM((MY_ROWS, WIDTH), BF),
     ]
     return tuple(pl.pallas_call(
         kernel,
@@ -460,7 +490,7 @@
             pltpu.VMEM((WIDTH, 3 * WIDTH), BF),
             pltpu.VMEM((WIDTH, WIDTH), BF),
         ]
-        + stage_buffers * 2
+        + stage_buffers
         + [
             pltpu.VMEM((HALF, LANES), BF),
             pltpu.VMEM((HALF, LANES), BF),
@@ -471,11 +501,8 @@
             pltpu.VMEM((1, ROWS), F32),
             pltpu.VMEM((1, ROWS), F32),
             pltpu.VMEM((LANES, ROWS), F32),
-            pltpu.VMEM((MY_ROWS, WIDTH), F32),
-            pltpu.VMEM((MY_ROWS, WIDTH), F32),
             dma((6,)),
             dma((3,)),
-            dma((2,)),
             dma((2, 2)),
             dma((2,)),
             dma((2, SUB)),

time: 70 us -> 69.7 us (level)
  no operation moved by 1% of the time
where the time goes in v4:
time: 69.7 us; the launch traced here: 69.6 us
  Pallas kernels  67.6 us (97%)
  local copies, waits for them, and re-layouts  1.31 us (2%)
    pallas_call x1, Pallas kernels, per_device(): pl.pallas_call(kernel, out_shape=(pltpu.VMEM((1, MY_ROWS, WIDTH), F32), p...  67.6 us

profile of v4, /device:TPU:1, one launch (start us, length us, event | category | flops | bytes accessed | tf_op | source)
XLA Modules:
  0.0 69.6 jit_solution(14649172969515913816)
XLA Ops:
  0.6 67.6 %shard_map.104 = (f32[1,32,1024]{2,1,0:T(8,128)S(1)}, f32[1,32,1024]{2,1,0:T(8,128)S(1)}) custom-call(s32[1,7]{1,0:T(1,128)} %nbr_hbm.1, bf16[1,32,1024]{2,1,0:T(8,128)(2,1)} %q1.1, bf16[1,32,1024]{2,1,0:T(8,128)(2,1)} %k1.1, bf16[1,32,1024]{2,1,0:T(8,128)(2,1)} %v1.1, bf16[1,32,1024]{2,1,0:T(8,128)(2,1)} %x2.1, bf16[1024,1024]{1,0:T(8,128)(2,1)} %w_view_out.1, ...), custom_call_target="tpu_custom_call" | custom-call | tf_op jit(solution)/shard_map/pallas_call | solution.py:477
  68.3 0.7 copy.13
  68.9 0.7 copy.14

commit v5 on v4

--- a/solution.py
+++ b/solution.py
@@ -26,6 +26,7 @@
 VIEWS = 2 * Z
 SUB = 4
 PIECE = ROWS // SUB
+TWICE = 1
 EXP2_SCALE = HD ** (-0.5) * math.log2(math.e)
 
 
@@ -127,6 +128,8 @@
     pl.semaphore_signal(barrier, inc=1, device_id=(right, tok), device_id_type=MESH)
     pl.semaphore_signal(barrier, inc=1, device_id=(left, tok), device_id_type=MESH)
     pl.semaphore_signal(barrier, inc=1, device_id=(view, partner), device_id_type=MESH)
+    pl.semaphore_signal(barrier, inc=1, device_id=(right, partner), device_id_type=MESH)
+    pl.semaphore_signal(barrier, inc=1, device_id=(left, partner), device_id_type=MESH)
 
     for copy in weights:
         copy.start()
@@ -204,14 +207,14 @@
             device_id_type=MESH,
         ).start()
 
-    def to_partner(stage, kv, from_z, sub, slot):
+    def to_partner(stage, kv, from_z, sub, slot, chip=None):
         block = rows_of(kv, (from_z * 2 + core) * ROWS + sub * PIECE, PIECE)
         pltpu.make_async_remote_copy(
             src_ref=block,
             dst_ref=block,
             send_sem=pair_send.at[stage],
             recv_sem=pair_recv.at[stage, slot],
-            device_id=(view, partner),
+            device_id=(view if chip is None else chip, partner),
             device_id_type=MESH,
         ).start()
 
@@ -281,12 +284,21 @@
             def _():
                 ring_piece(stage, kv, 1, step, sub)
 
+            for direction, from_z, chip in ((0, right_z, right), (1, left_z, left)):
+                end = SUB // 2 * (direction + 1)
+
+                @pl.when(jnp.logical_and(step == Z // 2 - 1, jnp.logical_and(sub >= end - TWICE, sub < end)))
+                def _():
+                    to_partner(stage, kv, from_z, sub, Z - 1, chip)
+
             to_partner(stage, kv, right_z, sub, 2 * step - 1)
             to_partner(stage, kv, left_z, sub, 2 * step)
 
         def last_pieces(sub):
             for direction, piece in ((0, sub), (1, SUB // 2 + sub)):
-                to_partner(stage, kv, piece_of(Z // 2, piece, direction), piece, Z - 1)
+                from_z = piece_of(Z // 2, piece, direction)
+                if sub < SUB // 2 - TWICE:
+                    to_partner(stage, kv, from_z, piece, Z - 1)
 
         def view_of(chip_z, whose):
             return chip_z * 2 + core + whose * (1 - 2 * core)
@@ -336,9 +348,9 @@
         last_pieces(0)
         last_pieces(1)
         score(kv, view_of(far, 0), *a)
-        weigh(kv, view_of(far, 0), *a)
         from_partner(view_of(far, 1), Z - 1)
         score(kv, view_of(far, 1), *b)
+        weigh(kv, view_of(far, 0), *a)
         weigh(kv, view_of(far, 1), *b)
 
     def ring_sent(stage, kv):
@@ -387,7 +399,7 @@
     for copy in loads[:2]:
         copy.wait()
     pack_keys(cut(k_in), cut(v_in), skvs.at[0])
-    pl.semaphore_wait(barrier, jnp.where(at_home, 2 * TOKS + 1, 2 * TOKS + 3))
+    pl.semaphore_wait(barrier, jnp.where(at_home, 2 * TOKS + 3, 2 * TOKS + 5))
 
     def attention(stage, _):
         sq, skv, rq, kv, so, ro = (ref.at[stage] for ref in (sqs, skvs, rqs, kvs, sos, ros))

time: 69.7 us -> 69.1 us (level)
  no operation moved by 1% of the time
where the time goes in v5:
time: 69.1 us; the launch traced here: 69 us
  Pallas kernels  67 us (97%)
  local copies, waits for them, and re-layouts  1.31 us (2%)
    pallas_call x1, Pallas kernels, per_device(): pl.pallas_call(kernel, out_shape=(pltpu.VMEM((1, MY_ROWS, WIDTH), F32), p...  67 us

profile of v5, /device:TPU:1, one launch (start us, length us, event | category | flops | bytes accessed | tf_op | source)
XLA Modules:
  0.0 69.0 jit_solution(14681226394806409911)
XLA Ops:
  0.6 67.0 %shard_map.104 = (f32[1,32,1024]{2,1,0:T(8,128)S(1)}, f32[1,32,1024]{2,1,0:T(8,128)S(1)}) custom-call(s32[1,7]{1,0:T(1,128)} %nbr_hbm.1, bf16[1,32,1024]{2,1,0:T(8,128)(2,1)} %q1.1, bf16[1,32,1024]{2,1,0:T(8,128)(2,1)} %k1.1, bf16[1,32,1024]{2,1,0:T(8,128)(2,1)} %v1.1, bf16[1,32,1024]{2,1,0:T(8,128)(2,1)} %x2.1, bf16[1024,1024]{1,0:T(8,128)(2,1)} %w_view_out.1, ...), custom_call_target="tpu_custom_call" | custom-call | tf_op jit(solution)/shard_map/pallas_call | solution.py:489
  67.7 0.7 copy.13
  68.3 0.7 copy.14

commit v6 on v5

--- a/solution.py
+++ b/solution.py
@@ -26,7 +26,7 @@
 VIEWS = 2 * Z
 SUB = 4
 PIECE = ROWS // SUB
-TWICE = 1
+TWICE = 2
 EXP2_SCALE = HD ** (-0.5) * math.log2(math.e)
 
 

time: 69.1 us -> 68.6 us (level)
  no operation moved by 1% of the time
where the time goes in v6:
time: 68.6 us; the launch traced here: 68.5 us
  Pallas kernels  66.5 us (97%)
  local copies, waits for them, and re-layouts  1.31 us (2%)
    pallas_call x1, Pallas kernels, per_device(): pl.pallas_call(kernel, out_shape=(pltpu.VMEM((1, MY_ROWS, WIDTH), F32), p...  66.5 us

profile of v6, /device:TPU:1, one launch (start us, length us, event | category | flops | bytes accessed | tf_op | source)
XLA Modules:
  0.0 68.5 jit_solution(5882058737697575353)
XLA Ops:
  0.6 66.5 %shard_map.104 = (f32[1,32,1024]{2,1,0:T(8,128)S(1)}, f32[1,32,1024]{2,1,0:T(8,128)S(1)}) custom-call(s32[1,7]{1,0:T(1,128)} %nbr_hbm.1, bf16[1,32,1024]{2,1,0:T(8,128)(2,1)} %q1.1, bf16[1,32,1024]{2,1,0:T(8,128)(2,1)} %k1.1, bf16[1,32,1024]{2,1,0:T(8,128)(2,1)} %v1.1, bf16[1,32,1024]{2,1,0:T(8,128)(2,1)} %x2.1, bf16[1024,1024]{1,0:T(8,128)(2,1)} %w_view_out.1, ...), custom_call_target="tpu_custom_call" | custom-call | tf_op jit(solution)/shard_map/pallas_call | solution.py:489
  67.1 0.7 copy.13
  67.8 0.7 copy.14
